TPU v7x, 32 devices: a whole 2x2x4 slice. The times are simulated.
32 devices in a mesh: dp: 16 (over z, x, core), mod: 2 (over y).
Axes of the slice: x: 2, y: 2, z: 4, core: 2. Of those that a mesh axis runs over, the one named last changes fastest.
Arguments:
- x_in: bfloat16 [32768, 1152], P(('dp', 'mod')), may hold values from -6 to 6
- cond: bfloat16 [128, 1152], P('dp'), may hold values from -4 to 4
- segments: int32 [32768], P(('dp', 'mod')), may hold values from 0 to 3, as said below
- out_grad: bfloat16 [32768, 1152], P(('dp', 'mod')), may hold values from -6 to 6
- qkv_weight: float32 [1152, 3456], P('dp', 'mod'), may hold values from -0.11785113 to 0.11785113
- qkv_moment: float32 [1152, 3456], P('dp', 'mod'), may hold values from -448 to 448
- qkv_average: float32 [1152, 3456], P('dp', 'mod'), may hold values from -0.1875 to 0.1875
- proj_weight: float32 [1152, 1152], P('dp', 'mod'), may hold values from -0.375 to 0.375
- proj_moment: float32 [1152, 1152], P('dp', 'mod'), may hold values from -448 to 448
- proj_average: float32 [1152, 1152], P('dp', 'mod'), may hold values from -0.375 to 0.375
- fc1_weight: float32 [1152, 4608], P('dp', 'mod'), may hold values from -0.1875 to 0.1875
- fc1_moment: float32 [1152, 4608], P('dp', 'mod'), may hold values from -320 to 320
- fc1_average: float32 [1152, 4608], P('dp', 'mod'), may hold values from -0.1875 to 0.1875
- fc2_weight: float32 [4608, 1152], P('dp', 'mod'), may hold values from -0.09375 to 0.09375
- fc2_moment: float32 [4608, 1152], P('dp', 'mod'), may hold values from -384 to 384
- fc2_average: float32 [4608, 1152], P('dp', 'mod'), may hold values from -0.09375 to 0.09375
- bias_weight: float32 [9216], P(('dp', 'mod')), may hold values from -1.25 to 1.25
- bias_moment: float32 [9216], P(('dp', 'mod')), may hold values from -896 to 896
- bias_average: float32 [9216], P(('dp', 'mod')), may hold values from -1.25 to 1.25
- ada_weight: float32 [1152, 6912], P('dp', 'mod'), may hold values from -0.11785113 to 0.11785113
- ada_moment: float32 [1152, 6912], P('dp', 'mod'), may hold values from -512 to 512
- ada_average: float32 [1152, 6912], P('dp', 'mod'), may hold values from -0.1875 to 0.1875
- adab_weight: float32 [2, 3456], P('mod', 'dp'), may hold values from -0.8 to 0.8
- adab_moment: float32 [2, 3456], P('mod', 'dp'), may hold values from -768 to 768
- adab_average: float32 [2, 3456], P('mod', 'dp'), may hold values from -1.25 to 1.25
Outputs:
- block_out: bfloat16 [32768, 1152], P(('dp', 'mod'))
- x_grad: float32 [32768, 1152], P(('dp', 'mod'))
- cond_grad: float32 [128, 1152], P('dp')
- qkv_weight_next: float32 [1152, 3456], P('dp', 'mod')
- qkv_moment_next: float32 [1152, 3456], P('dp', 'mod')
- qkv_average_next: float32 [1152, 3456], P('dp', 'mod')
- proj_weight_next: float32 [1152, 1152], P('dp', 'mod')
- proj_moment_next: float32 [1152, 1152], P('dp', 'mod')
- proj_average_next: float32 [1152, 1152], P('dp', 'mod')
- fc1_weight_next: float32 [1152, 4608], P('dp', 'mod')
- fc1_moment_next: float32 [1152, 4608], P('dp', 'mod')
- fc1_average_next: float32 [1152, 4608], P('dp', 'mod')
- fc2_weight_next: float32 [4608, 1152], P('dp', 'mod')
- fc2_moment_next: float32 [4608, 1152], P('dp', 'mod')
- fc2_average_next: float32 [4608, 1152], P('dp', 'mod')
- bias_weight_next: float32 [9216], P(('dp', 'mod'))
- bias_moment_next: float32 [9216], P(('dp', 'mod'))
- bias_average_next: float32 [9216], P(('dp', 'mod'))
- ada_weight_next: float32 [1152, 6912], P('dp', 'mod')
- ada_moment_next: float32 [1152, 6912], P('dp', 'mod')
- ada_average_next: float32 [1152, 6912], P('dp', 'mod')
- adab_weight_next: float32 [2, 3456], P('mod', 'dp')
- adab_moment_next: float32 [2, 3456], P('mod', 'dp')
- adab_average_next: float32 [2, 3456], P('mod', 'dp')
Inputs may be any that keep to these rules, and one draw needn't show every extreme that they name: `segments`: each aligned block of 1024 tokens of one device holds either one image, all of whose tokens carry the slot number of the block's first 256 tokens, or 4 images of 256 tokens, each token carrying its position within the device's tokens // 256. Both kinds occur in every draw.
All inputs are finite; a program needn't handle non-finite values.
Results may differ from a plain program's by a relative error of at most 0.013.
Values may be sent and summed in bfloat16 or wider, within the bound.
A program may use at most 384 MiB of HBM per device.

v0:
```python
from functools import partial

import jax
import jax.numpy as jnp
from jax import lax
from jax.experimental import pallas as pl
from jax.experimental.pallas import tpu as pltpu
from jax.sharding import Mesh
from jax.sharding import PartitionSpec as P

D = 1152
HEADS = 16
HEAD = 72
FF = 4608
LANES = 128
CHUNK = 256

ROWS = ("far", "near", "core")
ALL = ("far", "near", "core", "mod")
LOW = jnp.bfloat16
WIDE = jnp.float32
LOG2E = 1.4426950408889634
NEG = -1e30
MESH = pl.DeviceIdType.MESH
VMEM = pl.BlockSpec(memory_space=pltpu.VMEM)
ANY = pl.BlockSpec(memory_space=pl.ANY)

EPS = 1e-06
MOMENTUM = 0.9
DECAY = 0.5


def step_rates(tokens_all):
    base_rate = tokens_all ** (-0.5)
    return (
        2.5 * D ** (-0.5) * base_rate,
        3.0 * D ** (-0.5) * base_rate,
        3.3 * D ** (-0.5) * base_rate,
        2.8 * FF ** (-0.5) * base_rate,
        0.5 * base_rate,
        2.0 * D ** (-0.5) * base_rate,
        0.3 * base_rate,
    )


def nesterov(weight, moment, average, gradient, rate):
    moment = MOMENTUM * moment + gradient
    weight = weight - rate * (gradient + MOMENTUM * moment)
    average = DECAY * average + (1.0 - DECAY) * weight
    return (weight, moment, average)


def places():
    return {name: lax.axis_index(name) for name in ALL}


def greet():
    here = places()
    count = lax.axis_size("far")
    others = [dict(far=lax.rem(here["far"] + d, count)) for d in range(1, count)]
    others += [{name: 1 - here[name]} for name in ("near", "core", "mod")]
    barrier = pltpu.get_barrier_semaphore()
    for other in others:
        pl.semaphore_signal(barrier, inc=1, device_id=other, device_id_type=MESH)
    pl.semaphore_wait(barrier, len(others))


def remote(source, target, sends, receives, slot, other):
    return pltpu.make_async_remote_copy(
        src_ref=source,
        dst_ref=target,
        send_sem=sends.at[slot],
        recv_sem=receives.at[slot],
        device_id=other,
        device_id_type=MESH,
    )


def messages(count):
    return count - 1 + 8


class Gather:
    def __init__(self, whole, sends, receives):
        self.whole, self.sends, self.receives = whole, sends, receives
        self.here = places()
        self.count = lax.axis_size("far")
        rows = whole.shape[4]
        self.rows = rows
        self.split = rows if rows % 8 else 8 * ((rows // 8 + 1) // 2)

    def _block(self, far):
        return self.whole.at[self.here["mod"], far, self.here["near"], self.here["core"]]

    def _far(self, shard, distance):
        far = self.here["far"]
        other = dict(far=lax.rem(far + distance, self.count))
        return remote(shard, self._block(far), self.sends, self.receives, distance - 1, other)

    def _far_came(self, shard, distance):
        origin = lax.rem(self.here["far"] + self.count - distance, self.count)
        return remote(
            shard, self._block(origin), self.sends, self.receives, distance - 1, dict(far=origin)
        )

    def start_far(self, shard, local):
        pltpu.make_async_copy(shard, self._block(self.here["far"]), local).start()
        for distance in range(1, self.count):
            self._far(shard, distance).start()

    def finish_far(self, shard, local):
        pltpu.make_async_copy(shard, self._block(self.here["far"]), local).wait()
        for distance in range(1, self.count):
            self._far(shard, distance).wait_send()
            self._far_came(shard, distance).wait_recv()

    def _quad(self, flips, first, size):
        near, core, mod = (
            1 - self.here[name] if name in flips else self.here[name] for name in ("near", "core", "mod")
        )
        return self.whole.at[mod, :, near, core, pl.ds(first, size)]

    def _step(self, name):
        head, rest = (0, self.split), (self.split, self.rows - self.split)
        full = (0, self.rows)
        return {
            "near": ((), "near", full, 0),
            "mod": ((), "mod", full, 1),
            "near_mod": (("near",), "mod", head, 2),
            "mod_near": (("mod",), "near", rest, 3),
            "core": ((), "core", full, 4),
            "near_core": (("near",), "core", full, 5),
            "mod_core": (("mod",), "core", full, 6),
            "both_core": (("near", "mod"), "core", full, 7),
        }[name]

    def _copy(self, name, incoming):
        flips, axis, span, slot = self._step(name)
        if span[1] == 0:
            return None
        quad = self._quad(flips + (axis,) if incoming else flips, *span)
        other = {axis: 1 - self.here[axis]}
        return remote(quad, quad, self.sends, self.receives, self.count - 1 + slot, other)

    def start(self, *names):
        for name in names:
            copy = self._copy(name, False)
            if copy is not None:
                copy.start()

    def receive(self, *names):
        for name in names:
            copy = self._copy(name, True)
            if copy is not None:
                copy.wait_recv()

    def spread(self):
        self.start("near", "mod", "core")

    def cross(self):
        self.receive("near")
        self.start("near_mod", "near_core")
        self.receive("mod")
        self.start("mod_near", "mod_core")

    def close(self):
        self.receive("near_mod", "mod_near")
        self.start("both_core")

    def end(self):
        self.receive("core", "near_core", "mod_core", "both_core")
        for name in (
            "near", "mod", "near_mod", "mod_near", "core", "near_core", "mod_core", "both_core",
        ):
            copy = self._copy(name, False)
            if copy is not None:
                copy.wait_send()


def gather_scratch(weights, locals_):
    count = lax.axis_size("far")
    shapes = [pltpu.SemaphoreType.DMA((messages(count),))] * (2 * weights)
    return shapes + [pltpu.SemaphoreType.DMA((locals_,))]


def whole_shape(shard):
    return jax.ShapeDtypeStruct((2, lax.axis_size("far"), 2, 2) + shard.shape, LOW)


def modulate(small_w, ada, table, local, small, partials, came_core, came_near, came_far, own, sends, receives):
    here = places()
    count = lax.axis_size("far")
    far, near, core, mod = (here[name] for name in ALL)
    row_devices = 4 * count
    rows = D // row_devices
    fetch = pltpu.make_async_copy(small_w, small, local)
    fetch.start()
    fetch.wait()
    device = (far * 2 + near) * 2 + core
    half = lax.div(device, row_devices // 2)
    first = lax.rem(device, row_devices // 2) * rows
    width = small.shape[-1]
    images = small.shape[-2]
    row = lax.broadcasted_iota(jnp.int32, (width, LANES), 0)
    column = lax.broadcasted_iota(jnp.int32, (width, LANES), 1)
    select = jnp.where(jnp.logical_and(row == first + column, column < rows), 1.0, 0.0).astype(LOW)
    for at in range(count):
        silu = small[half, at].reshape(4 * images, width).astype(WIDE).astype(LOW)
        mine = times(silu, select)
        mine = jnp.where(lanes(mine.shape) == rows, 1.0, mine).astype(LOW)
        partials[at] = times(mine, ada[...]).reshape(2, 2, images, -1)

    def move(source, target, slot, other):
        return remote(source, target, sends, receives, slot, other)

    to_core = move(partials.at[:, :, 1 - core], came_core, 0, dict(core=1 - core))
    to_core.start()
    to_core.wait()
    for at in range(count):
        partials[at, :, core] = partials[at, :, core] + came_core[at]
    to_near = move(partials.at[:, 1 - near, core], came_near, 1, dict(near=1 - near))
    to_near.start()
    to_near.wait()
    for at in range(count):
        partials[at, near, core] = partials[at, near, core] + came_near[at]
    copies = []
    for distance in range(1, count):
        target = lax.rem(far + distance, count)
        copies.append(
            move(partials.at[target, near, core], came_far.at[distance - 1], 2 + distance, dict(far=target))
        )
        copies[-1].start()
    total = partials[far, near, core]
    for distance, copy in enumerate(copies):
        copy.wait()
        total = total + came_far[distance]
    own[...] = total.astype(LOW).astype(WIDE)
    keep = pltpu.make_async_copy(own, table.at[mod], local)
    keep.start()
    to_mod = move(own, table.at[mod], 2, dict(mod=1 - mod))
    to_mod.start()
    keep.wait()
    to_mod.wait_send()
    move(own, table.at[1 - mod], 2, dict(mod=1 - mod)).wait_recv()


def first_kernel(*refs):
    small_s, qkv_s, proj_s, fc1_s, ada = refs[:5]
    table = refs[9]
    gather_sems, (local, *parts) = refs[10:18], refs[18:]
    small, qkv, proj, fc1 = (
        Gather(w, s, r) for w, s, r in zip(refs[5:9], gather_sems[0::2], gather_sems[1::2])
    )
    greet()
    small.start_far(small_s, local.at[3])
    qkv.start_far(qkv_s, local.at[0])
    proj.start_far(proj_s, local.at[1])
    fc1.start_far(fc1_s, local.at[2])
    small.finish_far(small_s, local.at[3])
    small.spread()
    small.cross()
    small.close()
    small.end()
    modulate(small.whole, ada, table, local.at[3], *parts)
    qkv.finish_far(qkv_s, local.at[0])
    qkv.spread()
    qkv.cross()
    qkv.close()
    qkv.end()
    proj.finish_far(proj_s, local.at[1])
    fc1.finish_far(fc1_s, local.at[2])


def first_gather(ada, *shards):
    count = lax.axis_size("far")
    small = whole_shape(shards[0])
    images = small.shape[4]
    columns = ada.shape[1]
    return pl.pallas_call(
        first_kernel,
        out_shape=tuple(whole_shape(shard) for shard in shards)
        + (jax.ShapeDtypeStruct((2, images, columns), WIDE),),
        in_specs=[VMEM] * 5,
        out_specs=(ANY,) * 5,
        scratch_shapes=gather_scratch(4, 4)
        + [
            pltpu.VMEM(small.shape, LOW),
            pltpu.VMEM((count, 2, 2, images, columns), WIDE),
            pltpu.VMEM((count, 2, images, columns), WIDE),
            pltpu.VMEM((count, images, columns), WIDE),
            pltpu.VMEM((count - 1, images, columns), WIDE),
            pltpu.VMEM((images, columns), WIDE),
            pltpu.SemaphoreType.DMA((count + 2,)),
            pltpu.SemaphoreType.DMA((count + 2,)),
        ],
        compiler_params=pltpu.CompilerParams(
            collective_id=0, has_side_effects=True, vmem_limit_bytes=60 * 2**20
        ),
        name="first_gather",
    )(*shards, ada)


def lanes(shape): return lax.broadcasted_iota(jnp.int32, shape, 1)

def seg_codes(seg, n):
    lane = lanes((n, LANES))
    code = lane - HEAD
    inside = jnp.logical_and(code >= 0, code < 4)
    same = code == seg
    q = jnp.where(jnp.logical_and(inside, same), 1.0, 0.0)
    k = jnp.where(jnp.logical_and(inside, jnp.logical_not(same)), NEG, 0.0)
    return q, k

def head_of(wide_rows, start):
    return wide_rows[:, start:start+HEAD]

def pad_head(part, aug):
    n = part.shape[0]
    full = jnp.concatenate([part, jnp.zeros((n, LANES-HEAD), part.dtype)], axis=1)
    return jnp.where(lanes((n,LANES)) < HEAD, full, aug)

def attend_kernel(*refs):
    slots, x_ref, table, bias, weight, seg_ref, fc2_s = refs[:7]
    act_turned, joint_ref, mixed_ref, turned_ref, lse_ref, proj_w, fc1_w, fc2_w = refs[9:17]
    qh, kh, vh = refs[17:20]
    *sems, local = refs[20:]
    proj, fc1, fc2 = (
        Gather(w, s, r) for w, s, r in zip((proj_w, fc1_w, fc2_w), sems[0::2], sems[1::2])
    )
    greet()
    fc2.start_far(fc2_s, local.at[0])
    proj.spread()
    fc1.spread()

    T = x_ref.shape[0]

    def fill(i, carry):
        rows = pl.ds(pl.multiple_of(i * CHUNK, CHUNK), CHUNK)
        slot = slots[i]
        h1, _ = normed(x_ref[rows, :].astype(WIDE))
        act = (h1 * (1.0 + row_of(table, slot, 1)) + row_of(table, slot, 0)).astype(LOW)
        act_turned[:, rows] = act.T
        joint = jnp.concatenate([times(act, weight[0]), times(act, weight[1])], axis=1)
        joint_ref[rows, :] = (joint + bias[...]).astype(LOW)
        lane = lanes((CHUNK, LANES))
        qc, kc = seg_codes(seg_ref[rows, :], CHUNK)
        qc = qc.astype(LOW); kc = kc.astype(LOW)
        ones = jnp.where(jnp.logical_and(lane >= HEAD, lane < HEAD+3), 1.0, 0.0).astype(LOW)
        for h in range(HEADS):
            qh[h, rows, :] = pad_head(joint_ref[rows, h*HEAD:(h+1)*HEAD], qc)
            kh[h, rows, :] = pad_head(joint_ref[rows, D+h*HEAD:D+(h+1)*HEAD], kc)
            vh[h, rows, :] = pad_head(joint_ref[rows, 2*D+h*HEAD:2*D+(h+1)*HEAD], ones)
        return carry
    lax.fori_loop(0, T//CHUNK, fill, 0)
    lse_ref[...] = jnp.zeros_like(lse_ref)
    def head(h, carry):
        k = kh[h]; v = vh[h]
        for i in range(T//CHUNK):
            rows = pl.ds(i*CHUNK, CHUNK)
            q = qh[h, rows, :]
            s = lax.dot_general(q, k, (((1,),(1,)),((),())), preferred_element_type=WIDE)
            m = jnp.max(s, axis=1, keepdims=True)
            p = jnp.exp2((s - m)*(HEAD**-0.5*LOG2E)).astype(LOW)
            o = jnp.dot(p, v, preferred_element_type=WIDE)
            l = o[:, HEAD:HEAD+1]
            qh[h, rows, :] = (o / l).astype(LOW)
            col = m*HEAD**-0.5 + jnp.log(l)
            lse_ref[rows, :] = jnp.where(lanes((CHUNK,LANES)) == h, col, lse_ref[rows, :])
        tasks = {
            2: proj.cross,
            5: proj.close,
            7: proj.end,
            9: lambda: fc2.finish_far(fc2_s, local.at[0]),
            10: fc2.spread,
            11: fc1.cross,
        }
        for at, task in tasks.items():
            pl.when(h == at)(task)
        return carry
    lax.fori_loop(0, HEADS, head, 0)
    def drain(i, carry):
        rows = pl.ds(pl.multiple_of(i*CHUNK, CHUNK), CHUNK)
        mixed = jnp.concatenate([qh[h, rows, :][:, :HEAD] for h in range(HEADS)], axis=1)
        mixed_ref[rows, :] = mixed
        turned_ref[:, rows] = mixed.T
        return carry
    lax.fori_loop(0, T//CHUNK, drain, 0)
    fc1.close()
    fc2.cross()
    fc1.end()
    fc2.close()
    fc2.end()


def attend(slots, x_in, table, bias, weight, segments, fc2_s, proj_w, fc1_w):
    tokens = x_in.shape[0]
    wide = HEADS * HEAD
    return pl.pallas_call(
        attend_kernel,
        out_shape=(
            jax.ShapeDtypeStruct((wide, tokens), LOW),
            jax.ShapeDtypeStruct((tokens, 3 * wide), LOW),
            jax.ShapeDtypeStruct((tokens, wide), LOW),
            jax.ShapeDtypeStruct((wide, tokens), LOW),
            jax.ShapeDtypeStruct((tokens, LANES), WIDE),
            jax.ShapeDtypeStruct(proj_w.shape, LOW),
            jax.ShapeDtypeStruct(fc1_w.shape, LOW),
            whole_shape(fc2_s),
        ),
        in_specs=[pl.BlockSpec(memory_space=pltpu.SMEM)] + [VMEM] * 6 + [ANY] * 2,
        out_specs=(VMEM,) * 5 + (ANY,) * 3,
        scratch_shapes=[pltpu.VMEM((HEADS, tokens, LANES), LOW)] * 3 + gather_scratch(3, 1),
        input_output_aliases={7: 5, 8: 6},
        compiler_params=pltpu.CompilerParams(
            collective_id=1, has_side_effects=True, vmem_limit_bytes=60 * 2**20
        ),
        name="attend",
    )(slots, x_in, table, bias, weight, segments.reshape(tokens, 1), fc2_s, proj_w, fc1_w)


def row_spans(rows):
    first = rows if rows % 8 else 8 * ((rows // 8 + 1) // 2)
    return [(0, first)] + ([(first, rows - first)] if first < rows else [])


class Reduce:
    def __init__(self, part, span, first, came, joint, total, base, sems, loads=False):
        self.part, self.span, self.first = part, span, first
        self.second = "near" if first == "mod" else "mod"
        self.came_both, self.came_first, self.came_second, self.came_far = came
        self.joint, self.total_, self.base = joint, total, base
        self.sends, self.receives, self.locals_ = sems
        self.loads = loads
        self.here = places()
        self.count = lax.axis_size("far")

    def _swap(self, source, target, slot, axis):
        return remote(source, target, self.sends, self.receives, slot, {axis: 1 - self.here[axis]})

    def _both(self):
        return self._swap(self.part("near", "mod"), self.came_both, 0, self.first)

    def _first(self):
        return self._swap(self.part(self.first), self.came_first, 1, self.first)

    def _second(self):
        return self._swap(self.joint, self.came_second, 2, self.second)

    def _load(self, number):
        source, target = ((self.part(self.second), self.joint), (self.part(), self.total_))[number]
        return pltpu.make_async_copy(source, target, self.locals_.at[number])

    def _far(self, distance):
        target = lax.rem(self.here["far"] + distance, self.count)
        return remote(
            self.total_.at[target],
            self.came_far.at[distance - 1],
            self.sends,
            self.receives,
            2 + distance,
            dict(far=target),
        )

    def start(self):
        self._both().start()
        self._first().start()
        if self.loads:
            self._load(0).start()
            self._load(1).start()

    def merge(self):
        if self.loads:
            self._load(0).wait()
        self._both().wait_recv()

        def add(at, carry):
            self.joint[at] = (self.joint[at].astype(WIDE) + self.came_both[at].astype(WIDE)).astype(LOW)
            return carry

        lax.fori_loop(0, self.count, add, 0)
        self._second().start()

    def total(self):
        if self.loads:
            self._load(1).wait()
        self._first().wait_recv()
        self._second().wait_recv()

        def add(at, carry):
            self.total_[at] = (
                self.base[at].astype(WIDE)
                + self.came_first[at].astype(WIDE)
                + self.came_second[at].astype(WIDE)
            ).astype(LOW)
            return carry

        lax.fori_loop(0, self.count, add, 0)
        self._both().wait_send()
        self._first().wait_send()
        self._second().wait_send()

    def start_far(self):
        for distance in range(1, self.count):
            self._far(distance).start()

    def final(self, out):
        value = self.total_[self.here["far"]].astype(WIDE)
        for distance in range(1, self.count):
            self._far(distance).wait_recv()
            value = value + self.came_far[distance - 1].astype(WIDE)
        out[pl.ds(*self.span), :] = value
        for distance in range(1, self.count):
            self._far(distance).wait_send()


ORDERS = ("mod", "near")


def run(parts, *names):
    for part in parts:
        for name in names:
            getattr(part, name)()


def span_part(sums, span):
    def part(*flips):
        near, mod = (
            1 - lax.axis_index(name) if name in flips else lax.axis_index(name) for name in ("near", "mod")
        )
        return sums.at[mod, near, :, pl.ds(*span)]

    return part


def take(scratch, number):
    return scratch[:number], scratch[number:]


def came_scratch(count, span, columns, far=True):
    block = (count, span[1], columns)
    shapes = [pltpu.VMEM(block, LOW)] * 3
    return shapes + ([pltpu.VMEM((count - 1,) + block[1:], LOW)] if far else [])


def sem_scratch(count):
    return [pltpu.SemaphoreType.DMA((count + 2,))] * 2 + [pltpu.SemaphoreType.DMA((2,))]


def loaded_scratch(shape, total=True):
    count, rows, columns = shape[2:]
    shapes = []
    for span in row_spans(rows):
        shapes += came_scratch(count, span, columns)
        shapes += [pltpu.VMEM((count, span[1], columns), LOW)] * (2 if total else 1)
        shapes += sem_scratch(count)
    return shapes


def loaded_reduces(sums, scratch, totals=None):
    reduces = []
    for number, span in enumerate(row_spans(sums.shape[3])):
        came, scratch = take(scratch, 4)
        (joint,), scratch = take(scratch, 1)
        if totals is None:
            (total,), scratch = take(scratch, 1)
        else:
            total = totals[number]
        sems, scratch = take(scratch, 3)
        reduces.append(
            Reduce(span_part(sums, span), span, ORDERS[number], came, joint, total, total, sems, True)
        )
    return reduces, scratch


def resident_scratch(shape, far=True):
    count, rows, columns = shape[2:]
    shapes = []
    for span in row_spans(rows):
        shapes += came_scratch(count, span, columns, far) + sem_scratch(count)
    return shapes


def resident_reduces(sums, scratch, totals=None):
    reduces = []
    for number, span in enumerate(row_spans(sums.shape[3])):
        came, scratch = take(scratch, 4 if totals is None else 3)
        sems, scratch = take(scratch, 3)
        part = span_part(sums, span)
        order = ORDERS[number]
        own = part()
        total = own if totals is None else totals[number]
        came = list(came) + [None] * (4 - len(came))
        joint = part("near" if order == "mod" else "mod")
        reduces.append(Reduce(part, span, order, came, joint, total, own, sems))
    return reduces, scratch


def far_scratch(totals):
    shapes = []
    for total in totals:
        count = total.shape[0]
        shapes += [pltpu.VMEM((count - 1,) + total.shape[1:], LOW)] + sem_scratch(count)[:2]
    return shapes


def far_reduces(totals, rows, scratch):
    reduces = []
    for total, span in zip(totals, row_spans(rows)):
        (came, sends, receives), scratch = take(scratch, 3)
        came = (None, None, None, came)
        reduces.append(Reduce(None, span, "mod", came, None, total, total, (sends, receives, None)))
    return reduces, scratch


class Product:
    def __init__(self, left, right, scratch):
        self.left, self.right = left, right
        self.rows_, self.sums, self.came, self.loads, self.sends, self.receives = scratch
        self.core = lax.axis_index("core")

    @staticmethod
    def scratch(count, rows, tokens, columns):
        sums = pltpu.VMEM((2, 2, count, rows, columns), LOW)
        sems = [pltpu.SemaphoreType.DMA((4,))] * 3
        return [pltpu.VMEM((4, count, rows, tokens), LOW), sums, sums] + sems

    def _load(self, near, own):
        core = self.core if own else 1 - self.core
        slot = 2 * own + near
        return pltpu.make_async_copy(
            self.left.at[:, near, core], self.rows_.at[slot], self.loads.at[slot]
        )

    def load(self):
        for own in (0, 1):
            for near in (0, 1):
                self._load(near, own).start()

    def _copy(self, mod, near):
        return remote(
            self.sums.at[mod, near],
            self.came.at[mod, near],
            self.sends,
            self.receives,
            2 * mod + near,
            dict(core=1 - self.core),
        )

    def _blocks(self, near, own, store):
        count, rows, tokens = self.rows_.shape[1:]
        columns = self.right.shape[2]
        self._load(near, own).wait()
        left = self.rows_[2 * own + near].reshape(count * rows, tokens)
        width = columns if columns <= 1024 else columns // 2
        width = width if width % LANES == 0 else columns
        for mod in (0, 1):
            for at in range(0, columns, width):
                product = times(left, self.right[mod, :, at : at + width])
                store(mod, at, width, product.reshape(count, rows, width))

    def send(self):
        for near in (0, 1):

            def store(mod, at, width, product, near=near):
                self.sums[mod, near, :, :, at : at + width] = product.astype(LOW)

            self._blocks(near, 0, store)
            for mod in (0, 1):
                self._copy(mod, near).start()

    def sum(self):
        for near in (0, 1):
            for mod in (0, 1):
                self._copy(mod, near).wait_send()
                self._copy(mod, near).wait_recv()

            def store(mod, at, width, product, near=near):
                came = self.came[mod, near, :, :, at : at + width]
                self.sums[mod, near, :, :, at : at + width] = (product + came.astype(WIDE)).astype(LOW)

            self._blocks(near, 1, store)


def total_shapes(count, rows, columns):
    return [jax.ShapeDtypeStruct((count, span[1], columns), LOW) for span in row_spans(rows)]


def weight_kernel(*refs, spans, stored):
    count = stored + (spans > 0)
    sides, refs = take(refs, 2 * count)
    outs, refs = take(refs, stored)
    totals, scratch = take(refs, spans)
    products = []
    for number in range(count):
        used, scratch = take(scratch, 6)
        products.append(Product(sides[2 * number], sides[2 * number + 1], used))
    reduces = []
    if spans:
        reduces, scratch = resident_reduces(products[0].sums, scratch, totals)
    (out_sems,) = scratch
    products[0].load()
    greet()
    copies = []
    for number, product in enumerate(products):
        product.send()
        if number + 1 < count:
            products[number + 1].load()
        product.sum()
        if spans and number == 0:
            run(reduces, "start")
            continue
        copy = pltpu.make_async_copy(product.sums, outs[len(copies)], out_sems.at[len(copies)])
        copy.start()
        copies.append(copy)
        if spans and number == 1:
            run(reduces, "merge")
    if spans and count == 1:
        run(reduces, "merge")
    run(reduces, "total")
    for copy in copies:
        copy.wait()


def weight_call(summed, stored, number):
    pairs = summed + stored
    count, _, _, rows, tokens = pairs[0][0].shape
    columns = pairs[0][1].shape[2]
    totals = total_shapes(count, rows, columns) if summed else []
    scratch = []
    for left, right in pairs:
        scratch += Product.scratch(count, left.shape[3], tokens, right.shape[2])
    if summed:
        scratch += resident_scratch((2, 2, count, rows, columns), False)
    out = pl.pallas_call(
        partial(weight_kernel, spans=len(totals), stored=len(stored)),
        out_shape=tuple(
            jax.ShapeDtypeStruct((2, 2, count, left.shape[3], right.shape[2]), LOW) for left, right in stored
        )
        + tuple(totals),
        in_specs=[ANY, VMEM] * len(pairs),
        out_specs=(ANY,) * len(stored) + (VMEM,) * len(totals),
        scratch_shapes=scratch + [pltpu.SemaphoreType.DMA((2,))],
        compiler_params=pltpu.CompilerParams(
            collective_id=number, has_side_effects=True, vmem_limit_bytes=63 * 2**20
        ),
        name="weight_grads",
    )(*[side for pair in pairs for side in pair])
    return out[: len(stored)], out[len(stored) :]


def weight_grads(hidden, branch, mlp, pre, mixed, attn):
    summed, stored = [(hidden, branch)], [(mlp, pre), (mixed, attn)]
    if mlp.shape[3] % 8 == 0:
        return weight_call(summed, stored, 4)
    _, totals = weight_call(summed, [], 4)
    sums, _ = weight_call([], stored, 5)
    return sums, totals


def tile_sums_by_slot(chooser, sums):
    total = None
    for at, row in enumerate(sums):
        part = chooser[:, at : at + 1] * row
        total = part if total is None else total + part
    return total


def last_kernel(*refs, spans):
    slots, act, joint, x_ref, dx1_ref, table, weight, mid_sums, chooser = refs[:9]
    totals, refs = take(refs[9:], spans)
    qkv_out, fc1_out, small_w, x_grad_ref, joint_sums, *scratch = refs
    qkv_scratch, scratch = take(scratch, 6)
    qkv = Product(act, joint, qkv_scratch)
    qkv_sum, scratch = resident_reduces(qkv.sums, scratch)
    fc1_sum, scratch = far_reduces(totals, fc1_out.shape[0], scratch)
    small_sends, small_receives, local, first_sums, small_s = scratch
    small = Gather(small_w, small_sends, small_receives)
    tiles = x_ref.shape[0] // CHUNK
    qkv.load()
    greet()
    run(fc1_sum, "start_far")
    qkv.send()
    qkv.sum()
    run(qkv_sum, "start")

    def back(at, carry):
        rows = pl.ds(pl.multiple_of(at * CHUNK, CHUNK), CHUNK)
        dact = times_across(joint[0, rows, :], weight[0]) + times_across(joint[1, rows, :], weight[1])
        h1, inverse = normed(x_ref[rows, :].astype(WIDE))
        first_sums[at, 0:1, :] = column_sums(dact)
        first_sums[at, 1:2, :] = column_sums(dact * h1)
        dh1 = dact * (1.0 + row_of(table, slots[at], 1))
        x_grad_ref[rows, :] = dx1_ref[rows, :] + inverse * (
            dh1
            - jnp.mean(dh1, axis=-1, keepdims=True)
            - h1 * jnp.mean(dh1 * h1, axis=-1, keepdims=True)
        )
        for side in range(2):
            joint_sums[side : side + 1, :] += column_sums(joint[side, rows, :].astype(WIDE))

        @pl.when(at == tiles // 2 - 1)
        def _():
            run(qkv_sum, "merge")

        return carry

    joint_sums[...] = jnp.zeros_like(joint_sums)
    lax.fori_loop(0, tiles, back, 0)
    choose = chooser[...]
    upper = lax.broadcasted_iota(jnp.int32, (choose.shape[0], D), 0) < choose.shape[0] // 2
    groups = (
        [first_sums[at, 0:1, :] for at in range(tiles)],
        [first_sums[at, 1:2, :] for at in range(tiles)],
    ) + tuple([mid_sums[at, row : row + 1, :] for at in range(tiles)] for row in range(4))
    for group in range(3):
        value = jnp.where(
            upper, tile_sums_by_slot(choose, groups[group]), tile_sums_by_slot(choose, groups[group + 3])
        )
        small_s[:, group * D : (group + 1) * D] = value.astype(LOW)
    small.start_far(small_s, local.at[0])
    small.finish_far(small_s, local.at[0])
    small.spread()
    small.cross()
    small.close()
    small.end()
    run(qkv_sum, "total", "start_far")
    for part in fc1_sum:
        part.final(fc1_out)
    for part in qkv_sum:
        part.final(qkv_out)


def last_scatter(slots, act, joint, x_in, dx1, table, weight, mid_sums, chooser, totals):
    count, _, _, rows, tokens = act.shape
    fc1_columns = totals[0].shape[2]
    columns = joint.shape[2]
    small_s = jax.ShapeDtypeStruct((chooser.shape[0], 3 * D), LOW)
    return pl.pallas_call(
        partial(last_kernel, spans=len(totals)),
        out_shape=(
            jax.ShapeDtypeStruct((rows, columns), WIDE),
            jax.ShapeDtypeStruct((sum(total.shape[1] for total in totals), fc1_columns), WIDE),
            whole_shape(small_s),
            jax.ShapeDtypeStruct((tokens, D), WIDE),
            jax.ShapeDtypeStruct((2, columns), WIDE),
        ),
        in_specs=[pl.BlockSpec(memory_space=pltpu.SMEM), ANY] + [VMEM] * (7 + len(totals)),
        out_specs=(VMEM, VMEM, ANY, VMEM, VMEM),
        scratch_shapes=Product.scratch(count, rows, tokens, columns)
        + resident_scratch((2, 2, count, rows, columns))
        + far_scratch(totals)
        + gather_scratch(1, 1)
        + [pltpu.VMEM((tokens // CHUNK, 8, D), WIDE), pltpu.VMEM(small_s.shape, LOW)],
        compiler_params=pltpu.CompilerParams(
            collective_id=3, has_side_effects=True, vmem_limit_bytes=63 * 2**20
        ),
        name="last_scatter",
    )(slots, act, joint, x_in, dx1, table, weight, mid_sums, chooser, *totals)


def split3(v):
    hi = v.astype(LOW).astype(WIDE)
    mid = (v - hi).astype(LOW).astype(WIDE)
    lo = v - hi - mid
    return hi, mid, lo


def attend_back_kernel(*refs, fc2_spans, spans):
    qkv_ref, seg_ref, mixed_ref, lse_ref, up_ref, fc1_sums, proj_sums = refs[:7]
    fc2_totals, refs = take(refs[7:], fc2_spans)
    out_ref, fc2_out, proj_out, *refs = refs
    fc1_totals, refs = take(refs, spans)
    qh, kh, vh, uh, stage, stage_sems, leave, leave_sems, *scratch = refs
    proj, scratch = loaded_reduces(proj_sums, scratch)
    fc1, scratch = loaded_reduces(fc1_sums, scratch, fc1_totals)
    fc2, scratch = far_reduces(fc2_totals, fc2_out.shape[0], scratch)
    T = mixed_ref.shape[0]
    chunks = T // CHUNK
    greet()
    run(fc2, "start_far")
    run(fc1, "start")

    def load(i):
        rows = pl.ds(pl.multiple_of(i * CHUNK, CHUNK), CHUNK)
        slot = lax.rem(i, 2)
        return pltpu.make_async_copy(qkv_ref.at[rows], stage.at[slot], stage_sems.at[slot])

    load(0).start()

    def fill(i, carry):
        rows = pl.ds(pl.multiple_of(i * CHUNK, CHUNK), CHUNK)

        @pl.when(i + 1 < chunks)
        def _():
            load(i + 1).start()

        load(i).wait()
        qkv = stage.at[lax.rem(i, 2)]
        lane = lanes((CHUNK, LANES))
        qc, kc = seg_codes(seg_ref[rows, :], CHUNK)
        kc = jnp.where(jnp.logical_and(lane >= HEAD + 4, lane < HEAD + 7), 1.0, kc).astype(LOW)
        ones = jnp.where(jnp.logical_and(lane >= HEAD, lane < HEAD + 3), 1.0, 0.0).astype(LOW)

        def spread(v, at, base):
            hi, mid, lo = split3(v)
            return jnp.where(
                lane == at, hi, jnp.where(lane == at + 1, mid, jnp.where(lane == at + 2, lo, base))
            )

        for h in range(HEADS):
            a, b = h * HEAD, (h + 1) * HEAD
            qa = spread(-lse_ref[rows, h : h + 1] * HEAD**0.5, HEAD + 4, qc).astype(LOW)
            qh[h, rows, :] = pad_head(qkv[:, a:b], qa)
            kh[h, rows, :] = pad_head(qkv[:, D + a : D + b], kc)
            vh[h, rows, :] = pad_head(qkv[:, 2 * D + a : 2 * D + b], ones)
            u = up_ref[rows, a:b]
            delta = jnp.sum(u.astype(WIDE) * mixed_ref[rows, a:b].astype(WIDE), axis=1, keepdims=True)
            ua = spread(-delta, HEAD, jnp.zeros((CHUNK, LANES), WIDE)).astype(LOW)
            uh[h, rows, :] = pad_head(u, ua)
        return carry

    lax.fori_loop(0, chunks, fill, 0)
    across = (((1,), (1,)), ((), ()))
    tasks = {
        4: lambda: (run(fc1, "merge"), run(proj, "start")),
        11: lambda: run(proj, "merge"),
        14: lambda: run(proj, "total", "start_far"),
    }

    def head(h, carry):
        k = kh[h]
        v = vh[h]
        kt = k.T
        dk = jnp.zeros((T, LANES), WIDE)
        dv = jnp.zeros((T, LANES), WIDE)
        for i in range(chunks):
            rows = pl.ds(i * CHUNK, CHUNK)
            q = qh[h, rows, :]
            u = uh[h, rows, :]
            s = lax.dot_general(k, q, across, preferred_element_type=WIDE)
            p = jnp.exp2(s * (HEAD**-0.5 * LOG2E))
            dp = lax.dot_general(v, u, across, preferred_element_type=WIDE)
            ds = (p * dp).astype(LOW)
            dv = dv + jnp.dot(p.astype(LOW), u, preferred_element_type=WIDE)
            dk = dk + jnp.dot(ds, q, preferred_element_type=WIDE)
            dqt = jnp.dot(kt, ds, preferred_element_type=WIDE)
            qh[h, rows, :] = (dqt.T * HEAD**-0.5).astype(LOW)
        kh[h] = (dk * HEAD**-0.5).astype(LOW)
        vh[h] = dv.astype(LOW)
        for at, task in tasks.items():

            @pl.when(h == at)
            def _(task=task):
                task()

        return carry

    lax.fori_loop(0, HEADS, head, 0)

    def store(i, side):
        rows = pl.ds(pl.multiple_of(i * CHUNK, CHUNK), CHUNK)
        return pltpu.make_async_copy(
            leave.at[side], out_ref.at[side, rows], leave_sems.at[side]
        )

    def drain(i, carry):
        rows = pl.ds(pl.multiple_of(i * CHUNK, CHUNK), CHUNK)
        parts = [g[h, rows, :][:, :HEAD] for g in (qh, kh, vh) for h in range(HEADS)]
        for side in range(2):

            @pl.when(i > 0)
            def _(side=side):
                store(i - 1, side).wait()

            own = parts[side * len(parts) // 2 : (side + 1) * len(parts) // 2]
            leave[side] = jnp.concatenate(own, axis=1)
            store(i, side).start()
        return carry

    lax.fori_loop(0, chunks, drain, 0)
    run(fc1, "total")
    for side in range(2):
        store(chunks - 1, side).wait()
    for part in fc2:
        part.final(fc2_out)
    for part in proj:
        part.final(proj_out)


def attend_back(qkv, segments, mixed, lse, upstream, fc1_sums, proj_sums, fc2_totals):
    tokens = qkv.shape[0]
    count, rows, columns = fc1_sums.shape[2:]
    totals = total_shapes(count, rows, columns)
    fc2_rows = sum(total.shape[1] for total in fc2_totals)
    out = pl.pallas_call(
        partial(attend_back_kernel, fc2_spans=len(fc2_totals), spans=len(totals)),
        out_shape=(
            jax.ShapeDtypeStruct((2, tokens, 3 * HEADS * HEAD // 2), LOW),
            jax.ShapeDtypeStruct((fc2_rows, fc2_totals[0].shape[2]), WIDE),
            jax.ShapeDtypeStruct(proj_sums.shape[3:], WIDE),
        )
        + tuple(totals),
        in_specs=[ANY] + [VMEM] * 4 + [ANY] * 2 + [VMEM] * len(fc2_totals),
        out_specs=(ANY, VMEM, VMEM) + (VMEM,) * len(totals),
        scratch_shapes=[pltpu.VMEM((HEADS, tokens, LANES), LOW)] * 4
        + [pltpu.VMEM((2, CHUNK, 3 * HEADS * HEAD), LOW), pltpu.SemaphoreType.DMA((2,))]
        + [pltpu.VMEM((2, CHUNK, 3 * HEADS * HEAD // 2), LOW), pltpu.SemaphoreType.DMA((2,))]
        + loaded_scratch(proj_sums.shape)
        + loaded_scratch(fc1_sums.shape, False)
        + far_scratch(fc2_totals),
        compiler_params=pltpu.CompilerParams(
            collective_id=2, has_side_effects=True, vmem_limit_bytes=63 * 2**20
        ),
        name="attend_back",
    )(qkv, segments.reshape(tokens, 1), mixed, lse, upstream, fc1_sums, proj_sums, *fc2_totals)
    return out[0], out[1], out[2], out[3:]


def normed(values):
    centre = values - jnp.mean(values, axis=-1, keepdims=True)
    inverse = lax.rsqrt(jnp.mean(centre * centre, axis=-1, keepdims=True) + EPS)
    return centre * inverse, inverse


def row_of(table, slot, group):
    return table[pl.ds(slot, 1), group * D : (group + 1) * D]


def column_sums(values):
    return jnp.sum(values, axis=0, keepdims=True)


def times_across(left, right):
    return lax.dot_general(left, right, (((1,), (1,)), ((), ())), preferred_element_type=WIDE)


def fixed(*shape):
    return pl.BlockSpec(
        shape, lambda i, slots: (0,) * len(shape), pipeline_mode=pl.Buffered(1)
    )


GELU = 0.7978845608028654
CUBIC = 0.044715
SPAN = 768
BLOCK = 512


def middle_kernel(
    slots, x_ref, g_ref, mixed_ref, table, bias, bias1, proj, fc1, fc2,
    block_ref, mlp_turned, hidden_turned, dpre_ref, dbranch_ref, dattn_ref, dmixed_ref, dx1_ref, sums_ref, dpre_sums,
    attn_out, mlp, branch,
):
    step = pl.program_id(0)
    tokens = x_ref.shape[0]

    @pl.when(step == 0)
    def _():
        def enter(tile_at, carry):
            rows = pl.ds(pl.multiple_of(tile_at * CHUNK, CHUNK), CHUNK)
            slot = slots[tile_at]
            gate1, shift2, scale2, gate2 = (row_of(table, slot, group) for group in (2, 3, 4, 5))
            mixed = mixed_ref[rows, :]
            out = jnp.concatenate([times(mixed, proj[0]), times(mixed, proj[1])], axis=1)
            out = out + bias[:, 2 * D : 3 * D]
            attn_out[rows, :] = out
            h2, _ = normed(x_ref[rows, :].astype(WIDE) + gate1 * out)
            mlp_in = (h2 * (1.0 + scale2) + shift2).astype(LOW)
            mlp[rows, :] = mlp_in
            mlp_turned[:, rows] = mlp_in.T
            dbranch = (gate2 * g_ref[rows, :].astype(WIDE)).astype(LOW)
            sums_ref[tile_at, 5:6, :] = column_sums(dbranch.astype(WIDE))
            dbranch_ref[0, rows, :] = dbranch[:, : D // 2]
            dbranch_ref[1, rows, :] = dbranch[:, D // 2 :]
            return carry

        lax.fori_loop(0, tokens // CHUNK, enter, 0)
        branch[...] = jnp.zeros_like(branch)
        dx1_ref[...] = jnp.zeros_like(dx1_ref)

    total = None
    for first in range(0, tokens, BLOCK):
        rows = slice(first, first + BLOCK)
        pre = times(mlp[rows, :], fc1[0]) + bias1[0]
        square = pre * pre
        bend = jnp.tanh(GELU * pre * (1.0 + CUBIC * square))
        rise = 0.5 * (1.0 + bend)
        hidden = (pre * rise).astype(LOW)
        hidden_turned[:, rows] = hidden.T
        for side in range(2):
            branch[side, rows] += times(hidden, fc2[side])
        slope = rise + 0.5 * GELU * pre * (1.0 - bend * bend) * (1.0 + 3.0 * CUBIC * square)
        dhidden = times_across(dbranch_ref[0, rows], fc2[0]) + times_across(dbranch_ref[1, rows], fc2[1])
        dpre = (dhidden * slope).astype(LOW)
        dpre_ref[0, rows] = dpre
        part = column_sums(dpre.astype(WIDE))
        total = part if total is None else total + part
        dx1_ref[rows, :] += times_across(dpre, fc1[0])
    dpre_sums[...] = total

    @pl.when(step == pl.num_programs(0) - 1)
    def _():
        def leave(tile_at, carry):
            rows = pl.ds(pl.multiple_of(tile_at * CHUNK, CHUNK), CHUNK)
            slot = slots[tile_at]
            gate1, scale2, gate2 = (row_of(table, slot, group) for group in (2, 4, 5))
            out = attn_out[rows, :]
            x1 = x_ref[rows, :].astype(WIDE) + gate1 * out
            h2, inverse = normed(x1)
            whole = jnp.concatenate([branch[0, rows, :], branch[1, rows, :]], axis=1) + bias[:, 3 * D + FF :]
            block_ref[rows, :] = (x1 + gate2 * whole).astype(LOW)
            g = g_ref[rows, :].astype(WIDE)
            sums_ref[tile_at, 3:4, :] = column_sums(g * whole)
            dmlp = dx1_ref[rows, :]
            sums_ref[tile_at, 1:2, :] = column_sums(dmlp)
            sums_ref[tile_at, 2:3, :] = column_sums(dmlp * h2)
            dh2 = dmlp * (1.0 + scale2)
            dx1 = g + inverse * (
                dh2
                - jnp.mean(dh2, axis=-1, keepdims=True)
                - h2 * jnp.mean(dh2 * h2, axis=-1, keepdims=True)
            )
            dx1_ref[rows, :] = dx1
            sums_ref[tile_at, 0:1, :] = column_sums(dx1 * out)
            dattn = (gate1 * dx1).astype(LOW)
            sums_ref[tile_at, 4:5, :] = column_sums(dattn.astype(WIDE))
            sums_ref[tile_at, 6:8, :] = jnp.zeros((2, D), WIDE)
            left, right = dattn[:, : D // 2], dattn[:, D // 2 :]
            dattn_ref[0, rows, :] = left
            dattn_ref[1, rows, :] = right
            dmixed_ref[rows, :] = (times_across(left, proj[0]) + times_across(right, proj[1])).astype(LOW)
            return carry

        lax.fori_loop(0, tokens // CHUNK, leave, 0)


def middle(slots, x_in, out_grad, mixed, table, bias, proj, fc1, fc2):
    tokens = x_in.shape[0]
    tiles = tokens // CHUNK
    steps = FF // SPAN
    per_side = steps // 2
    bias1 = bias[:, 3 * D : 3 * D + FF].reshape(steps, 1, SPAN)

    def by_unit(shape, place):
        return pl.BlockSpec(shape, lambda j, slots: place(j))

    outs = (
        ((tokens, D), LOW),
        ((D, tokens), LOW),
        ((FF, tokens), LOW),
        ((2, tokens, FF // 2), LOW),
        ((2, tokens, D // 2), LOW),
        ((2, tokens, D // 2), LOW),
        ((tokens, D), LOW),
        ((tokens, D), WIDE),
        ((tiles, 8, D), WIDE),
        ((1, FF), WIDE),
    )
    out_specs = [fixed(*shape) for shape, _ in outs]
    out_specs[2] = by_unit((SPAN, tokens), lambda j: (j, 0))
    out_specs[3] = by_unit((1, tokens, SPAN), lambda j: (j // per_side, 0, j % per_side))
    out_specs[9] = by_unit((1, SPAN), lambda j: (0, j))
    return pl.pallas_call(
        middle_kernel,
        out_shape=tuple(jax.ShapeDtypeStruct(shape, dtype) for shape, dtype in outs),
        grid_spec=pltpu.PrefetchScalarGridSpec(
            num_scalar_prefetch=1,
            grid=(steps,),
            in_specs=[
                fixed(tokens, D),
                fixed(tokens, D),
                fixed(tokens, D),
                fixed(*table.shape),
                fixed(*bias.shape),
                by_unit((1, 1, SPAN), lambda j: (j, 0, 0)),
                fixed(*proj.shape),
                by_unit((1, D, SPAN), lambda j: (j // per_side, 0, j % per_side)),
                by_unit((2, SPAN, D // 2), lambda j: (0, j, 0)),
            ],
            out_specs=tuple(out_specs),
            scratch_shapes=[
                pltpu.VMEM((tokens, D), WIDE),
                pltpu.VMEM((tokens, D), LOW),
                pltpu.VMEM((2, tokens, D // 2), WIDE),
            ],
        ),
        compiler_params=pltpu.CompilerParams(
            dimension_semantics=("arbitrary",), vmem_limit_bytes=63 * 2**20
        ),
        cost_estimate=pl.CostEstimate(
            flops=4 * tokens * (D * D + 2 * D * FF),
            bytes_accessed=(D * D + 2 * D * FF) * 2 + tokens * D * 40,
            transcendentals=0,
        ),
        name="middle",
    )(slots, x_in, out_grad, mixed, table, bias, bias1, proj, fc1, fc2)


def swap(values, axis):
    return lax.ppermute(values, axis, [(0, 1), (1, 0)])


def times(left, right):
    return jnp.dot(left, right, preferred_element_type=WIDE)


def times_back(left, right):
    return lax.dot_general(left, right, (((1,), (1,)), ((), ())), preferred_element_type=WIDE)


def body(
    x_in,
    cond,
    segments,
    out_grad,
    qkv_weight,
    qkv_moment,
    qkv_average,
    proj_weight,
    proj_moment,
    proj_average,
    fc1_weight,
    fc1_moment,
    fc1_average,
    fc2_weight,
    fc2_moment,
    fc2_average,
    bias_weight,
    bias_moment,
    bias_average,
    ada_weight,
    ada_moment,
    ada_average,
    adab_weight,
    adab_moment,
    adab_average,
):
    tokens, width = x_in.shape
    row_devices = lax.axis_size(ROWS)
    devices = lax.axis_size(ALL)
    row_index = lax.axis_index(ROWS)
    images = cond.shape[0] // 2

    cond_silu, silu_back = jax.vjp(jax.nn.silu, cond.astype(WIDE))
    half_silu = lax.dynamic_index_in_dim(
        cond_silu.astype(LOW).reshape(-1, 2, width // 2), lax.axis_index("mod"), 1, False
    )
    own_bias = bias_weight.shape[0]
    bias_block = jnp.pad(bias_weight.astype(LOW), (0, 8 * LANES - own_bias)).reshape(8, LANES)
    blank = jnp.zeros((8, LANES // 2), LOW)
    ada_low = ada_weight.astype(LOW)
    adab_row = lax.dynamic_update_slice_in_dim(
        jnp.zeros((1, ada_weight.shape[1]), LOW),
        adab_weight.astype(LOW),
        row_index * adab_weight.shape[1],
        1,
    )
    ada_rows = jnp.concatenate([ada_low, adab_row])
    small_w, qkv_w, proj_w, fc1_w, table = first_gather(
        jnp.pad(ada_rows, ((0, LANES - ada_rows.shape[0]), (0, 0))),
        jnp.concatenate([half_silu, bias_block, blank], axis=1),
        qkv_weight.astype(LOW),
        proj_weight.astype(LOW),
        fc1_weight.astype(LOW),
    )
    small = small_w.reshape(2, row_devices * 8, -1)
    silu_all = jnp.concatenate([small[0, :, : width // 2], small[1, :, : width // 2]], axis=1)
    bias_all = small[:, :, width // 2 : width // 2 + LANES].reshape(2, row_devices, -1)
    bias_full = jnp.swapaxes(bias_all[:, :, :own_bias], 0, 1).reshape(1, -1).astype(WIDE)
    table = lax.dynamic_slice_in_dim(table, lax.axis_index("mod") * images, images, 1)
    table = jnp.swapaxes(table, 0, 1).reshape(images, -1)

    def joined(whole):
        return whole.reshape(2, -1, whole.shape[-1])

    qkv_low = joined(qkv_w)
    slots = segments[::CHUNK]
    joint_bias = jnp.concatenate(
        [bias_full[:, 0:width], jnp.zeros((1, width), WIDE), bias_full[:, width : 2 * width]], axis=1
    )
    def blocked(turned):
        return turned.reshape(row_devices // 4, 2, 2, -1, tokens)

    act_turned, joint_rows, mixture, mixture_turned, log_totals, proj_w, fc1_w, fc2_w = attend(
        slots,
        x_in,
        table,
        joint_bias,
        qkv_low,
        segments,
        fc2_weight.astype(LOW),
        proj_w,
        fc1_w,
    )
    (
        block_out, mlp_turned, hidden_turned, pre_halves, branch_halves, attn_halves, mixture_grad, middle_grad, sums, pre_sums,
    ) = middle(
        slots, x_in, out_grad, mixture, table, bias_full, joined(proj_w), joined(fc1_w), joined(fc2_w)
    )
    (fc1_sums, proj_sums), fc2_totals = weight_grads(
        blocked(hidden_turned),
        branch_halves,
        blocked(mlp_turned),
        pre_halves,
        blocked(mixture_turned),
        attn_halves,
    )
    joint_halves, fc2_shard, proj_shard, fc1_totals = attend_back(
        joint_rows,
        segments,
        mixture,
        log_totals,
        mixture_grad,
        fc1_sums,
        proj_sums,
        fc2_totals,
    )
    chooser = (slots[None, :] == (jnp.arange(2 * images, dtype=jnp.int32) % images)[:, None]).astype(WIDE)
    qkv_shard, fc1_shard, mod_grad_w, x_grad, joint_sums = last_scatter(
        slots,
        blocked(act_turned),
        joint_halves,
        x_in,
        middle_grad,
        table,
        qkv_low,
        sums,
        chooser,
        fc1_totals,
    )
    mod_grads = mod_grad_w.reshape(2, row_devices, 2, images, -1)
    mod_grads = lax.dynamic_index_in_dim(mod_grads, lax.axis_index("mod"), 2, False)
    mod_grad_all = jnp.swapaxes(mod_grads, 0, 1).reshape(2 * row_devices * images, -1)
    own_rows = ada_weight.shape[0]
    own_silu = lax.dynamic_slice_in_dim(silu_all, row_index * own_rows, own_rows, 1)
    ada_shard = jnp.einsum("ic,io->co", own_silu, mod_grad_all, preferred_element_type=WIDE)
    own_columns = adab_weight.shape[1]
    adab_shard = jnp.sum(
        lax.dynamic_slice_in_dim(mod_grad_all, row_index * own_columns, own_columns, 1).astype(WIDE),
        axis=0,
    )
    silu_part = times_back(mod_grad_all, ada_low)
    silu_part = lax.all_to_all(silu_part, ROWS, split_axis=0, concat_axis=1, tiled=True)
    cond_grad = silu_back(silu_part + swap(silu_part, "mod"))[0]

    joint_sum = joint_sums.reshape(-1)
    sum_rows = jnp.sum(sums, axis=0)
    grad_bias = jnp.concatenate(
        [
            joint_sum[0:width],
            joint_sum[2 * width :],
            sum_rows[4],
            pre_sums.reshape(-1),
            sum_rows[5],
        ]
    ).reshape(devices, -1)
    bias_shard = jnp.sum(
        lax.all_to_all(grad_bias, ALL, split_axis=0, concat_axis=0, tiled=True), axis=0
    )

    rates = step_rates(tokens * devices)
    states_out = []
    states_out.extend(nesterov(qkv_weight, qkv_moment, qkv_average, qkv_shard, rates[0]))
    states_out.extend(nesterov(proj_weight, proj_moment, proj_average, proj_shard, rates[1]))
    states_out.extend(nesterov(fc1_weight, fc1_moment, fc1_average, fc1_shard, rates[2]))
    states_out.extend(nesterov(fc2_weight, fc2_moment, fc2_average, fc2_shard, rates[3]))
    states_out.extend(nesterov(bias_weight, bias_moment, bias_average, bias_shard, rates[4]))
    states_out.extend(nesterov(ada_weight, ada_moment, ada_average, ada_shard, rates[5]))
    states_out.extend(
        nesterov(adab_weight, adab_moment, adab_average, adab_shard.reshape(1, -1), rates[6])
    )
    return (block_out, x_grad, cond_grad) + tuple(states_out)


def solution(mesh):
    far = mesh.shape["dp"] // 4
    fine = Mesh(mesh.devices.reshape(far, 2, 2, mesh.shape["mod"]), ALL)
    tokens = P(ALL, None)
    images = P(ROWS, None)
    trunk = P(ROWS, "mod")
    bias = P(ALL)
    adab = P("mod", ROWS)
    states = (trunk,) * 12 + (bias,) * 3 + (trunk,) * 3 + (adab,) * 3
    return jax.shard_map(
        body,
        mesh=fine,
        in_specs=(tokens, images, bias, tokens) + states,
        out_specs=(tokens, tokens, images) + states,
        check_vma=False,
    )
```

profile of v0, /device:TPU:0, one launch (start us, length us, event | category | flops | bytes accessed | tf_op | source)
XLA Modules:
  0.0 669.2 jit_solution(7378847500565012348)
XLA Ops:
  0.7 0.8 convert_element_type.46
  1.5 0.7 convert_element_type.51
  2.1 0.7 fusion.9
  3.0 1.6 convert_element_type.48.refs_2_
  4.6 1.8 convert_element_type.47.refs_1_
  6.4 1.9 convert_element_type.49.refs_3_
  8.4 0.2 dynamic_update_slice.3
  8.6 1.0 fusion.2.refs_4_
  9.6 0.7 maximum_maximum_fusion.refs_0_
  10.2 117.6 %first_gather.1 = (bf16[2,4,2,2,8,768]{5,4,3,2,1,0:T(8,128)(2,1)}, bf16[2,4,2,2,72,1728]{5,4,3,2,1,0:T(8,128)(2,1)}, bf16[2,4,2,2,72,576]{5,4,3,2,1,0:T(8,128)(2...) custom-call(bf16[8,768]{1,0:T(8,128)(2,1)} %maximum_maximum_fusion.refs_0_, ...), custom_call_target="tpu_custom_call" | custom-call | tf_op jit(solution)/shard_map/first_gather/pallas_call | solution.py:279
  127.9 1.0 slice.48
  128.9 0.1 reshape.163.bias
  129.1 0.6 slice.52
  129.8 0.8 convert_element_type.55.refs_6_
  130.6 1.0 copy.77.refs_5_.refs_1_
  131.6 0.7 compare_convert_fusion.refs_8_
  132.3 1.6 constant_dynamic-slice_fusion.1
  133.9 0.6 fusion.15.refs_3_
  134.5 137.8 %attend.1 = (bf16[1152,1024]{1,0:T(8,128)(2,1)}, bf16[1024,3456]{1,0:T(8,128)(2,1)}, bf16[1024,1152]{1,0:T(8,128)(2,1)}, bf16[1152,1024]{1,0:T(8,128)(2,1)}, f32...) custom-call(s32[4]{0:T(128)} %copy-done.24, ...), custom_call_target="tpu_custom_call", output_to_operand_aliasing={{5}: (7, {}), {6}: (8, {})} | custom-call | tf_op jit(solution)/shard_map/attend/pallas_call | solution.py:398
  272.4 98.8 %middle.1 = (bf16[1024,1152]{1,0:T(8,128)(2,1)}, bf16[1152,1024]{1,0:T(8,128)(2,1)}, bf16[4608,1024]{1,0:T(8,128)(2,1)}, bf16[2,1024,2304]{2,1,0:T(8,128)(2,1)},...) custom-call(s32[4]{0:T(128)} %copy-done.24, ...), custom_call_target="tpu_custom_call" | custom-call | flops 48922361856 | bytes 71073792 | tf_op jit(solution)/shard_map/middle/pallas_call | solution.py:1163
  371.1 76.3 %weight_grads.1 = (bf16[2,2,4,72,2304]{4,3,2,1,0:T(8,128)(2,1)}, bf16[2,2,4,72,576]{4,3,2,1,0:T(8,128)(2,1)}, bf16[4,144,576]{2,1,0:T(8,128)(2,1)}, bf16[4,144,576]{2,1,0:T(8,128)(2,1)}) custom-call(bf16[4,2,2,288,1024]{4,3,2,1,0:T(8,128)(2,1)} %bitcast.43, bf16[2,1024,576]{2,1,0:T(8,128)(2,1)} %get-tuple-element.76.refs_1_, ...), custom_call_target="tpu_custom_call" | custom-call | tf_op jit(solution)/shard_map/weight_grads/pallas_call | solution.py:734
  447.4 82.1 %attend_back.1 = (bf16[2,1024,1728]{2,1,0:T(8,128)(2,1)}, f32[288,576]{1,0:T(8,128)}, f32[72,576]{1,0:T(8,128)}, bf16[4,40,2304]{2,1,0:T(8,128)(2,1)}, bf16[4,32,2304]{2,1,0:T(8,128)(2,1)}) custom-call(bf16[1024,3456]{1,0:T(8,128)(2,1)} %get-tuple-element.72.refs_0_, s32[1024,1]{1,0:T(8,128)} %copy.77.refs_5_.refs_1_, ...), custom_call_target="tpu_custom_call" | custom-call | tf_op jit(solution)/shard_map/attend_back/pallas_call | solution.py:995
  529.5 95.1 %last_scatter.1 = (f32[72,1728]{1,0:T(8,128)}, f32[72,2304]{1,0:T(8,128)}, bf16[2,4,2,2,8,3456]{5,4,3,2,1,0:T(8,128)(2,1)}, f32[1024,1152]{1,0:T(8,128)}, f32[2,1728]{1,0:T(2,128)}) custom-call(s32[4]{0:T(128)} %copy-done.24, bf16[4,2,2,72,1024]{4,3,2,1,0:T(8,128)(2,1)} %bitcast.47, bf16[2,1024,1728]{2,1,0:T(8,128)(2,1)} %get-tuple-element.85.refs_2_, ...), custom_call_target="tpu_custom_call" | custom-call | tf_op jit(solution)/shard_map/last_scatter/pallas_call | solution.py:838
  624.6 3.3 reshape.158
  627.9 0.3 constant_dynamic-slice_fusion
  628.3 0.6 copy-done.6
  628.9 1.0 fusion.3
  629.9 5.8 all-to-all-start
  635.7 0.7 slice_bitcast_fusion
  636.6 0.3 copy.83
  636.9 0.2 reshape.161
  637.3 2.1 add_multiply_fusion.4
  639.4 2.6 add_multiply_fusion.3
  642.0 1.5 add_multiply_fusion.2
  643.5 0.2 copy-done.10
  643.8 0.5 copy-done.11
  644.3 1.5 add_multiply_fusion.1
  645.8 0.7 copy-done.7
  646.6 0.3 copy-done.8
  647.0 2.2 add_multiply_fusion
  649.2 0.7 all_to_all.21
  650.1 5.4 all-to-all-start.1
  655.5 0.6 add_multiply_fusion.6
  656.1 1.8 collective-permute-start
  658.0 4.9 all-to-all-done.1
  663.0 0.6 add_multiply_fusion.5
  663.6 0.6 fusion.11
  664.2 4.8 copy.104
  (90 shorter events, 1.2 us)
Async XLA Ops:
  0.7 7.6 %copy-start = (f32[72,3456]{1,0:T(8,128)S(1)}, f32[72,3456]{1,0:T(8,128)}, u32[]{:S(2)}) copy-start(f32[72,3456]{1,0:T(8,128)} %param.44) | copy-start | bytes 2985988
  8.2 121.5 %copy-start.25 = (s32[1024]{0:T(1024)S(1)}, s32[1024]{0:T(1024)}, u32[]{:S(2)}) copy-start(s32[1024]{0:T(1024)} %param.27) | copy-start | bytes 12292
  8.2 121.6 %copy-start.2 = (f32[288,576]{1,0:T(8,128)S(1)}, f32[288,576]{1,0:T(8,128)}, u32[]{:S(2)}) copy-start(f32[288,576]{1,0:T(8,128)} %param.38) | copy-start | bytes 1990660
  8.3 122.3 %copy-start.5 = (bf16[72,3456]{1,0:T(8,128)(2,1)}, bf16[72,3456]{1,0:T(8,128)(2,1)S(1)}, u32[]{:S(2)}) copy-start(bf16[72,3456]{1,0:T(8,128)(2,1)S(1)} %convert_element_type.50) | copy-start | bytes 1492996
  129.1 143.3 %copy-start.19 = (f32[1,9216]{1,0:T(1,128)}, f32[1,9216]{1,0:T(1,128)S(1)}, u32[]{:S(2)}) copy-start(f32[1,9216]{1,0:T(1,128)S(1)} %reshape.163.bias) | copy-start | bytes 110596
  129.8 4.7 copy-start.24
  627.8 1.0 copy-start.6
  628.2 7.5 %copy-start.18 = (bf16[2,4,2,2,8,768]{5,4,3,2,1,0:T(8,128)(2,1)S(1)}, bf16[2,4,2,2,8,768]{5,4,3,2,1,0:T(8,128)(2,1)}, u32[]{:S(2)}) copy-start(bf16[2,4,2,2,8,768]{5,4,3,2,1,0:T(8,128)(2,1)} %get-tuple-element.62) | copy-start | bytes 1179652
  628.2 8.2 %copy-start.17 = (f32[4,8,1152]{2,1,0:T(8,128)S(1)}, f32[4,8,1152]{2,1,0:T(8,128)}, u32[]{:S(2)}) copy-start(f32[4,8,1152]{2,1,0:T(8,128)} %get-tuple-element.87.refs_7_) | copy-start | bytes 442372
  628.2 8.3 %copy-start.22 = (f32[2,1728]{1,0:T(2,128)S(1)}, f32[2,1728]{1,0:T(2,128)}, u32[]{:S(2)}) copy-start(f32[2,1728]{1,0:T(2,128)} %get-tuple-element.96) | copy-start | bytes 41476
  629.9 7.2 %copy-start.21 = (f32[1,4608]{1,0:T(1,128)S(1)}, f32[1,4608]{1,0:T(1,128)}, u32[]{:S(2)}) copy-start(f32[1,4608]{1,0:T(1,128)} %get-tuple-element.97) | copy-start | bytes 55300
  629.9 7.3 %copy-start.12 = (f32[72,576]{1,0:T(8,128)S(1)}, f32[72,576]{1,0:T(8,128)}, u32[]{:S(2)}) copy-start(f32[72,576]{1,0:T(8,128)} %param.32) | copy-start | bytes 497668
  629.9 20.1 %all-to-all-start = ((f32[16,8,72]{2,1,0:T(8,128)}), f32[16,8,72]{2,1,0:T(8,128)S(1)}, u32[]{:S(2)}, u32[]{:S(2)}) async-start(f32[16,8,72]{2,1,0:T(8,128)} %fusion.3), calls=%async_computation | async-start | bytes 131072 | tf_op jit(solution)/shard_map/all_to_all | solution.py:1343
  636.6 2.8 copy-start.4
  637.3 4.8 copy-start.3
  637.3 4.8 copy-start.13
  637.3 4.7 copy-start.14
  637.3 4.7 copy-start.15
  642.0 1.5 copy-start.9
  642.0 1.8 copy-start.10
  642.0 2.3 copy-start.11
  644.3 1.6 copy-start.1
  644.3 2.3 copy-start.7
  644.3 2.6 copy-start.8
  644.3 2.6 copy-start.16
  646.9 8.5 %copy-start.26 = (f32[1,216]{1,0:T(1,128)S(1)}, f32[1,216]{1,0:T(1,128)}, u32[]{:S(2)}) copy-start(f32[1,216]{1,0:T(1,128)} %param.47) | copy-start | bytes 2596
  646.9 8.5 %copy-start.29 = (f32[1,216]{1,0:T(1,128)S(1)}, f32[1,216]{1,0:T(1,128)}, u32[]{:S(2)}) copy-start(f32[1,216]{1,0:T(1,128)} %param.49) | copy-start | bytes 2596
  646.9 8.5 %copy-start.30 = (f32[1,216]{1,0:T(1,128)S(1)}, f32[1,216]{1,0:T(1,128)}, u32[]{:S(2)}) copy-start(f32[1,216]{1,0:T(1,128)} %param.48) | copy-start | bytes 2596
  646.9 16.1 %copy-start.23 = (f32[288]{0:T(512)S(1)}, f32[288]{0:T(512)}, u32[]{:S(2)}) copy-start(f32[288]{0:T(512)} %param.41) | copy-start | bytes 3460
  646.9 16.1 %copy-start.27 = (f32[288]{0:T(512)S(1)}, f32[288]{0:T(512)}, u32[]{:S(2)}) copy-start(f32[288]{0:T(512)} %param.43) | copy-start | bytes 3460
  646.9 16.1 %copy-start.28 = (f32[288]{0:T(512)S(1)}, f32[288]{0:T(512)}, u32[]{:S(2)}) copy-start(f32[288]{0:T(512)} %param.42) | copy-start | bytes 3460
  646.9 16.7 %copy-start.20 = (bf16[8,1152]{1,0:T(8,128)(2,1)S(1)}, bf16[8,1152]{1,0:T(8,128)(2,1)}, u32[]{:S(2)}) copy-start(bf16[8,1152]{1,0:T(8,128)(2,1)} %param.26) | copy-start | bytes 55300
  650.1 12.8 %all-to-all-start.1 = ((f32[32,1,288]{2,1,0:T(1,128)}), f32[32,1,288]{2,1,0:T(1,128)S(1)}, u32[]{:S(2)}, u32[]{:S(2)}) async-start(f32[32,1,288]{2,1,0:T(1,128)} %all_to_all.21), calls=%async_computation.1 | async-start | bytes 98304 | tf_op jit(solution)/shard_map/all_to_all | solution.py:1358
  656.1 7.4 %collective-permute-start = (f32[8,1152]{1,0:T(8,128)S(1)}, f32[8,1152]{1,0:T(8,128)S(1)}, u32[]{:S(2)}, u32[]{:S(2)}) collective-permute-start(f32[8,1152]{1,0:T(8,128)S(1)} %all_to_all.20), channel_id=1, source_target_pairs={{0,1},{1,0},{2,3},{3,2},{4,5},{5,4},{6,7},{7,6},{8,9},{9,8},{10,11... | collective-permute-start | bytes 110600 | tf_op jit(solution)/shard_map/ppermute | solution.py:1200
where the time goes:
time: 677 us; the launch traced here: 669 us
  Pallas kernels  608 us (90%)
  other arithmetic  20.9 us (3%)
  local copies, waits for them, and re-layouts  18.1 us (3%)
  starting transfers between devices  13 us (2%)
    pallas_call x1, Pallas kernels, attend(): pl.pallas_call(attend_kernel, out_shape=(jax.ShapeDtypeStruct((wide, toke...  138 us
    pallas_call x1, Pallas kernels, first_gather(): pl.pallas_call(first_kernel, out_shape=tuple((whole_shape(shard) for shar...  118 us
    pallas_call x1, Pallas kernels, middle(): pl.pallas_call(middle_kernel, out_shape=tuple((jax.ShapeDtypeStruct(shape...  98.8 us
    pallas_call x1, Pallas kernels, last_scatter(): pl.pallas_call(partial(last_kernel, spans=len(totals)), out_shape=(jax.Sh...  95.1 us
    pallas_call x1, Pallas kernels, attend_back(): pl.pallas_call(partial(attend_back_kernel, fc2_spans=len(fc2_totals), spa...  82.1 us
    pallas_call x1, Pallas kernels, weight_call(): pl.pallas_call(partial(weight_kernel, spans=len(totals), stored=len(store...  76.3 us
  transfers between devices with their start and end apart: 3, of which 1 were waited for; matrix products, arithmetic and copies ran while one was open for 2% of the time, Pallas kernels for 0%

commit v1 on v0

--- a/solution.py
+++ b/solution.py
@@ -220,6 +220,7 @@
         partials[at, :, core] = partials[at, :, core] + came_core[at]
     to_near = move(partials.at[:, 1 - near, core], came_near, 1, dict(near=1 - near))
     to_near.start()
+    yield
     to_near.wait()
     for at in range(count):
         partials[at, near, core] = partials[at, near, core] + came_near[at]
@@ -230,6 +231,7 @@
             move(partials.at[target, near, core], came_far.at[distance - 1], 2 + distance, dict(far=target))
         )
         copies[-1].start()
+    yield
     total = partials[far, near, core]
     for distance, copy in enumerate(copies):
         copy.wait()
@@ -239,6 +241,7 @@
     keep.start()
     to_mod = move(own, table.at[mod], 2, dict(mod=1 - mod))
     to_mod.start()
+    yield
     keep.wait()
     to_mod.wait_send()
     move(own, table.at[1 - mod], 2, dict(mod=1 - mod)).wait_recv()
@@ -254,19 +257,23 @@
     greet()
     small.start_far(small_s, local.at[3])
     qkv.start_far(qkv_s, local.at[0])
-    proj.start_far(proj_s, local.at[1])
-    fc1.start_far(fc1_s, local.at[2])
     small.finish_far(small_s, local.at[3])
     small.spread()
     small.cross()
     small.close()
     small.end()
-    modulate(small.whole, ada, table, local.at[3], *parts)
+    stages = modulate(small.whole, ada, table, local.at[3], *parts)
+    next(stages)
     qkv.finish_far(qkv_s, local.at[0])
     qkv.spread()
+    next(stages)
+    proj.start_far(proj_s, local.at[1])
+    fc1.start_far(fc1_s, local.at[2])
+    next(stages)
     qkv.cross()
     qkv.close()
     qkv.end()
+    next(stages, None)
     proj.finish_far(proj_s, local.at[1])
     fc1.finish_far(fc1_s, local.at[2])
 
@@ -350,6 +357,7 @@
             qh[h, rows, :] = pad_head(joint_ref[rows, h*HEAD:(h+1)*HEAD], qc)
             kh[h, rows, :] = pad_head(joint_ref[rows, D+h*HEAD:D+(h+1)*HEAD], kc)
             vh[h, rows, :] = pad_head(joint_ref[rows, 2*D+h*HEAD:2*D+(h+1)*HEAD], ones)
+        pl.when(i == 2)(proj.cross)
         return carry
     lax.fori_loop(0, T//CHUNK, fill, 0)
     lse_ref[...] = jnp.zeros_like(lse_ref)
@@ -367,15 +375,17 @@
             col = m*HEAD**-0.5 + jnp.log(l)
             lse_ref[rows, :] = jnp.where(lanes((CHUNK,LANES)) == h, col, lse_ref[rows, :])
         tasks = {
-            2: proj.cross,
-            5: proj.close,
-            7: proj.end,
-            9: lambda: fc2.finish_far(fc2_s, local.at[0]),
-            10: fc2.spread,
-            11: fc1.cross,
+            3: lambda: (fc2.finish_far(fc2_s, local.at[0]), fc2.spread()),
+            6: fc1.cross,
+            8: proj.close,
+            10: proj.end,
         }
         for at, task in tasks.items():
-            pl.when(h == at)(task)
+
+            @pl.when(h == at)
+            def _(task=task):
+                task()
+
         return carry
     lax.fori_loop(0, HEADS, head, 0)
     def drain(i, carry):
@@ -385,8 +395,8 @@
         turned_ref[:, rows] = mixed.T
         return carry
     lax.fori_loop(0, T//CHUNK, drain, 0)
+    fc2.cross()
     fc1.close()
-    fc2.cross()
     fc1.end()
     fc2.close()
     fc2.end()
@@ -766,14 +776,14 @@
 
 
 def last_kernel(*refs, spans):
-    slots, act, joint, x_ref, dx1_ref, table, weight, mid_sums, chooser = refs[:9]
-    totals, refs = take(refs[9:], spans)
-    qkv_out, fc1_out, small_w, x_grad_ref, joint_sums, *scratch = refs
+    slots, act, joint, x_ref, dx1_ref, table, weight, mid_sums, pre_sums, chooser = refs[:10]
+    totals, refs = take(refs[10:], spans)
+    qkv_out, fc1_out, small_w, x_grad_ref, *scratch = refs
     qkv_scratch, scratch = take(scratch, 6)
     qkv = Product(act, joint, qkv_scratch)
     qkv_sum, scratch = resident_reduces(qkv.sums, scratch)
     fc1_sum, scratch = far_reduces(totals, fc1_out.shape[0], scratch)
-    small_sends, small_receives, local, first_sums, small_s = scratch
+    small_sends, small_receives, local, first_sums, joint_sums, small_s = scratch
     small = Gather(small_w, small_sends, small_receives)
     tiles = x_ref.shape[0] // CHUNK
     qkv.load()
@@ -816,25 +826,36 @@
         value = jnp.where(
             upper, tile_sums_by_slot(choose, groups[group]), tile_sums_by_slot(choose, groups[group + 3])
         )
-        small_s[:, group * D : (group + 1) * D] = value.astype(LOW)
+        small_s[0:8, group * D : (group + 1) * D] = value.astype(LOW)
+    pre = pre_sums[...]
+    tile_rows = [column_sums(mid_sums[:, row, :]) for row in (4, 5)]
+    biases = (
+        (joint_sums[0:1, :D], joint_sums[1:2, D // 2 :], tile_rows[0]),
+        tuple(pre[:, at * D : (at + 1) * D] for at in range(3)),
+        (pre[:, 3 * D :], tile_rows[1], jnp.zeros((1, D), WIDE)),
+    )
+    blank = jnp.zeros((5, D), WIDE)
+    for group in range(3):
+        rows = jnp.concatenate([biases[row][group] for row in range(3)] + [blank], axis=0)
+        small_s[8:16, group * D : (group + 1) * D] = rows.astype(LOW)
     small.start_far(small_s, local.at[0])
     small.finish_far(small_s, local.at[0])
     small.spread()
+    run(qkv_sum, "total", "start_far")
     small.cross()
     small.close()
     small.end()
-    run(qkv_sum, "total", "start_far")
     for part in fc1_sum:
         part.final(fc1_out)
     for part in qkv_sum:
         part.final(qkv_out)
 
 
-def last_scatter(slots, act, joint, x_in, dx1, table, weight, mid_sums, chooser, totals):
+def last_scatter(slots, act, joint, x_in, dx1, table, weight, mid_sums, pre_sums, chooser, totals):
     count, _, _, rows, tokens = act.shape
     fc1_columns = totals[0].shape[2]
     columns = joint.shape[2]
-    small_s = jax.ShapeDtypeStruct((chooser.shape[0], 3 * D), LOW)
+    small_s = jax.ShapeDtypeStruct((16, 3 * D), LOW)
     return pl.pallas_call(
         partial(last_kernel, spans=len(totals)),
         out_shape=(
@@ -842,20 +863,23 @@
             jax.ShapeDtypeStruct((sum(total.shape[1] for total in totals), fc1_columns), WIDE),
             whole_shape(small_s),
             jax.ShapeDtypeStruct((tokens, D), WIDE),
-            jax.ShapeDtypeStruct((2, columns), WIDE),
         ),
-        in_specs=[pl.BlockSpec(memory_space=pltpu.SMEM), ANY] + [VMEM] * (7 + len(totals)),
-        out_specs=(VMEM, VMEM, ANY, VMEM, VMEM),
+        in_specs=[pl.BlockSpec(memory_space=pltpu.SMEM), ANY] + [VMEM] * (8 + len(totals)),
+        out_specs=(VMEM, VMEM, ANY, VMEM),
         scratch_shapes=Product.scratch(count, rows, tokens, columns)
         + resident_scratch((2, 2, count, rows, columns))
         + far_scratch(totals)
         + gather_scratch(1, 1)
-        + [pltpu.VMEM((tokens // CHUNK, 8, D), WIDE), pltpu.VMEM(small_s.shape, LOW)],
+        + [
+            pltpu.VMEM((tokens // CHUNK, 8, D), WIDE),
+            pltpu.VMEM((2, columns), WIDE),
+            pltpu.VMEM(small_s.shape, LOW),
+        ],
         compiler_params=pltpu.CompilerParams(
             collective_id=3, has_side_effects=True, vmem_limit_bytes=63 * 2**20
         ),
         name="last_scatter",
-    )(slots, act, joint, x_in, dx1, table, weight, mid_sums, chooser, *totals)
+    )(slots, act, joint, x_in, dx1, table, weight, mid_sums, pre_sums, chooser, *totals)
 
 
 def split3(v):
@@ -1196,10 +1220,6 @@
     )(slots, x_in, out_grad, mixed, table, bias, bias1, proj, fc1, fc2)
 
 
-def swap(values, axis):
-    return lax.ppermute(values, axis, [(0, 1), (1, 0)])
-
-
 def times(left, right):
     return jnp.dot(left, right, preferred_element_type=WIDE)
 
@@ -1316,7 +1336,7 @@
         fc2_totals,
     )
     chooser = (slots[None, :] == (jnp.arange(2 * images, dtype=jnp.int32) % images)[:, None]).astype(WIDE)
-    qkv_shard, fc1_shard, mod_grad_w, x_grad, joint_sums = last_scatter(
+    qkv_shard, fc1_shard, small_grads, x_grad = last_scatter(
         slots,
         blocked(act_turned),
         joint_halves,
@@ -1325,12 +1345,16 @@
         table,
         qkv_low,
         sums,
+        pre_sums,
         chooser,
         fc1_totals,
     )
-    mod_grads = mod_grad_w.reshape(2, row_devices, 2, images, -1)
-    mod_grads = lax.dynamic_index_in_dim(mod_grads, lax.axis_index("mod"), 2, False)
+    small_grads = small_grads.reshape(2, row_devices, 16, -1)
+    mod_grads = lax.dynamic_slice_in_dim(small_grads, lax.axis_index("mod") * images, images, 2)
     mod_grad_all = jnp.swapaxes(mod_grads, 0, 1).reshape(2 * row_devices * images, -1)
+    bias_grads = small_grads[:, :, 8:11].reshape(devices, -1)
+    own_biases = lax.dynamic_slice_in_dim(bias_grads, lax.axis_index(ALL) * own_bias, own_bias, 1)
+    bias_shard = jnp.sum(own_biases.astype(WIDE), axis=0)
     own_rows = ada_weight.shape[0]
     own_silu = lax.dynamic_slice_in_dim(silu_all, row_index * own_rows, own_rows, 1)
     ada_shard = jnp.einsum("ic,io->co", own_silu, mod_grad_all, preferred_element_type=WIDE)
@@ -1340,23 +1364,13 @@
         axis=0,
     )
     silu_part = times_back(mod_grad_all, ada_low)
-    silu_part = lax.all_to_all(silu_part, ROWS, split_axis=0, concat_axis=1, tiled=True)
-    cond_grad = silu_back(silu_part + swap(silu_part, "mod"))[0]
-
-    joint_sum = joint_sums.reshape(-1)
-    sum_rows = jnp.sum(sums, axis=0)
-    grad_bias = jnp.concatenate(
-        [
-            joint_sum[0:width],
-            joint_sum[2 * width :],
-            sum_rows[4],
-            pre_sums.reshape(-1),
-            sum_rows[5],
-        ]
-    ).reshape(devices, -1)
-    bias_shard = jnp.sum(
-        lax.all_to_all(grad_bias, ALL, split_axis=0, concat_axis=0, tiled=True), axis=0
-    )
+    row_images = 2 * images
+    silu_part = jnp.broadcast_to(
+        silu_part.reshape(row_devices, 1, row_images, -1), (row_devices, 2, row_images, own_rows)
+    ).reshape(devices * row_images, own_rows)
+    silu_part = lax.all_to_all(silu_part, ALL, split_axis=0, concat_axis=1, tiled=True)
+    silu_grad = jnp.sum(silu_part.reshape(row_images, row_devices, 2, own_rows), axis=2)
+    cond_grad = silu_back(silu_grad.reshape(row_images, -1))[0]
 
     rates = step_rates(tokens * devices)
     states_out = []

time: 677 us -> 609 us (0.90)
  Pallas kernels: 608 us -> 552 us
  starting transfers between devices: 13 us -> 5.01 us
    pallas_call x1, Pallas kernels: 118 us -> 83.5 us  [first_gather(): pl.pallas_call(first_kernel, out_shape=tuple((whole_shape(shard) for shar...]
    pallas_call x1, Pallas kernels: 95.1 us -> 81.1 us  [last_scatter(): pl.pallas_call(partial(last_kernel, spans=len(totals)), out_shape=(jax.Sh...]
    pallas_call x1, Pallas kernels: 138 us -> 129 us  [attend(): pl.pallas_call(attend_kernel, out_shape=(jax.ShapeDtypeStruct((wide, toke...]
  transfers between devices with their start and end apart: 3 -> 1, of which waited for: 1 -> 0; matrix products, arithmetic and copies ran while one was open for 2% -> 3% of each run, Pallas kernels for 0% -> 0%
where the time goes in v1:
time: 609 us; the launch traced here: 602 us
  Pallas kernels  552 us (91%)
  other arithmetic  23.7 us (4%)
  local copies, waits for them, and re-layouts  17.3 us (3%)
    pallas_call x1, Pallas kernels, attend(): pl.pallas_call(attend_kernel, out_shape=(jax.ShapeDtypeStruct((wide, toke...  129 us
    pallas_call x1, Pallas kernels, middle(): pl.pallas_call(middle_kernel, out_shape=tuple((jax.ShapeDtypeStruct(shape...  99 us
    pallas_call x1, Pallas kernels, first_gather(): pl.pallas_call(first_kernel, out_shape=tuple((whole_shape(shard) for shar...  83.5 us
    pallas_call x1, Pallas kernels, attend_back(): pl.pallas_call(partial(attend_back_kernel, fc2_spans=len(fc2_totals), spa...  82.2 us
    pallas_call x1, Pallas kernels, last_scatter(): pl.pallas_call(partial(last_kernel, spans=len(totals)), out_shape=(jax.Sh...  81.1 us
    pallas_call x1, Pallas kernels, weight_call(): pl.pallas_call(partial(weight_kernel, spans=len(totals), stored=len(store...  77 us
  transfers between devices with their start and end apart: 1, of which 0 were waited for; matrix products, arithmetic and copies ran while one was open for 3% of the time, Pallas kernels for 0%

profile of v1, /device:TPU:0, one launch (start us, length us, event | category | flops | bytes accessed | tf_op | source)
XLA Modules:
  0.0 601.5 jit_solution(6661047513837387311)
XLA Ops:
  0.7 0.7 convert_element_type.49
  1.4 0.7 convert_element_type.54
  2.1 0.7 fusion.8
  3.0 1.6 convert_element_type.51.refs_2_
  4.5 1.8 convert_element_type.50.refs_1_
  6.3 1.9 convert_element_type.52.refs_3_
  8.2 1.3 convert_element_type.53
  9.6 0.2 dynamic_update_slice.3
  9.8 1.0 fusion.2.refs_4_
  10.7 0.7 maximum_maximum_fusion.refs_0_
  11.4 83.5 %first_gather.1 = (bf16[2,4,2,2,8,768]{5,4,3,2,1,0:T(8,128)(2,1)}, bf16[2,4,2,2,72,1728]{5,4,3,2,1,0:T(8,128)(2,1)}, bf16[2,4,2,2,72,576]{5,4,3,2,1,0:T(8,128)(2...) custom-call(bf16[8,768]{1,0:T(8,128)(2,1)} %maximum_maximum_fusion.refs_0_, ...), custom_call_target="tpu_custom_call" | custom-call | tf_op jit(solution)/shard_map/first_gather/pallas_call | solution.py:286
  95.0 1.0 slice.36
  96.0 0.1 reshape.174.bias
  96.2 0.6 slice.40
  96.9 0.8 convert_element_type.58.refs_6_
  97.7 1.0 copy.65.refs_5_.refs_1_
  98.7 0.7 compare_convert_fusion.refs_9_
  99.4 1.6 constant_dynamic-slice_fusion.1
  101.0 0.6 fusion.14.refs_3_
  101.6 128.8 %attend.1 = (bf16[1152,1024]{1,0:T(8,128)(2,1)}, bf16[1024,3456]{1,0:T(8,128)(2,1)}, bf16[1024,1152]{1,0:T(8,128)(2,1)}, bf16[1152,1024]{1,0:T(8,128)(2,1)}, f32...) custom-call(s32[4]{0:T(128)} %copy-done.19, ...), custom_call_target="tpu_custom_call", output_to_operand_aliasing={{5}: (7, {}), {6}: (8, {})} | custom-call | tf_op jit(solution)/shard_map/attend/pallas_call | solution.py:408
  230.4 99.0 %middle.1 = (bf16[1024,1152]{1,0:T(8,128)(2,1)}, bf16[1152,1024]{1,0:T(8,128)(2,1)}, bf16[4608,1024]{1,0:T(8,128)(2,1)}, bf16[2,1024,2304]{2,1,0:T(8,128)(2,1)},...) custom-call(s32[4]{0:T(128)} %copy-done.19, ...), custom_call_target="tpu_custom_call" | custom-call | flops 48922361856 | bytes 71073792 | tf_op jit(solution)/shard_map/middle/pallas_call | solution.py:1187
  329.4 77.0 %weight_grads.1 = (bf16[2,2,4,72,2304]{4,3,2,1,0:T(8,128)(2,1)}, bf16[2,2,4,72,576]{4,3,2,1,0:T(8,128)(2,1)}, bf16[4,144,576]{2,1,0:T(8,128)(2,1)}, bf16[4,144,576]{2,1,0:T(8,128)(2,1)}) custom-call(bf16[4,2,2,288,1024]{4,3,2,1,0:T(8,128)(2,1)} %bitcast.45, bf16[2,1024,576]{2,1,0:T(8,128)(2,1)} %get-tuple-element.75.refs_1_, ...), custom_call_target="tpu_custom_call" | custom-call | tf_op jit(solution)/shard_map/weight_grads/pallas_call | solution.py:744
  406.4 82.2 %attend_back.1 = (bf16[2,1024,1728]{2,1,0:T(8,128)(2,1)}, f32[288,576]{1,0:T(8,128)}, f32[72,576]{1,0:T(8,128)}, bf16[4,40,2304]{2,1,0:T(8,128)(2,1)}, bf16[4,32,2304]{2,1,0:T(8,128)(2,1)}) custom-call(bf16[1024,3456]{1,0:T(8,128)(2,1)} %get-tuple-element.71.refs_0_, s32[1024,1]{1,0:T(8,128)} %copy.65.refs_5_.refs_1_, ...), custom_call_target="tpu_custom_call" | custom-call | tf_op jit(solution)/shard_map/attend_back/pallas_call | solution.py:1019
  488.5 81.1 %last_scatter.1 = (f32[72,1728]{1,0:T(8,128)}, f32[72,2304]{1,0:T(8,128)}, bf16[2,4,2,2,16,3456]{5,4,3,2,1,0:T(8,128)(2,1)}, f32[1024,1152]{1,0:T(8,128)}) custom-call(s32[4]{0:T(128)} %copy-done.19, bf16[4,2,2,72,1024]{4,3,2,1,0:T(8,128)(2,1)} %bitcast.48, bf16[2,1024,1728]{2,1,0:T(8,128)(2,1)} %get-tuple-element.84.refs_2_, bf16[1024,1152]{1,0:T(8,128)(2,1)} %refs_3_.1, ...), custom_call_target="tpu_custom_call" | custom-call | tf_op jit(solution)/shard_map/last_scatter/pallas_call | solution.py:859
  569.7 2.0 copy_bitcast_fusion
  571.7 0.2 reshape.168
  571.9 0.4 fusion.3
  572.3 0.7 broadcast_in_dim.19
  573.0 5.0 all-to-all-start
  578.0 0.7 slice_bitcast_fusion
  578.7 1.8 slice.41
  580.5 0.2 reshape.172
  580.7 0.9 copy.71
  581.6 0.1 convert_reduce_fusion
  581.8 1.0 convert_reduce_fusion.1
  582.8 1.9 add_multiply_fusion.4
  584.7 0.6 add_multiply_fusion.5
  585.3 2.6 add_multiply_fusion.3
  588.0 1.5 add_multiply_fusion.2
  589.5 0.2 copy-done.7
  589.7 0.5 copy-done.8
  590.2 0.2 copy-done.9
  590.4 1.5 add_multiply_fusion.1
  592.0 2.2 add_multiply_fusion
  594.3 0.6 add_multiply_fusion.6
  594.9 0.9 bitcast_reduce_fusion
  595.9 0.6 fusion.10
  596.6 4.8 copy.79
  (67 shorter events, 0.6 us)
Async XLA Ops:
  6.3 90.5 %copy-start.20 = (s32[1024]{0:T(1024)S(1)}, s32[1024]{0:T(1024)}, u32[]{:S(2)}) copy-start(s32[1024]{0:T(1024)} %param.27) | copy-start | bytes 12292
  6.3 90.6 %copy-start.1 = (f32[288,576]{1,0:T(8,128)S(1)}, f32[288,576]{1,0:T(8,128)}, u32[]{:S(2)}) copy-start(f32[288,576]{1,0:T(8,128)} %param.38) | copy-start | bytes 1990660
  96.2 134.2 %copy-start.16 = (f32[1,9216]{1,0:T(1,128)}, f32[1,9216]{1,0:T(1,128)S(1)}, u32[]{:S(2)}) copy-start(f32[1,9216]{1,0:T(1,128)S(1)} %reshape.174.bias) | copy-start | bytes 110596
  96.9 4.7 copy-start.19
  569.7 8.3 %copy-start.15 = (bf16[2,4,2,2,8,768]{5,4,3,2,1,0:T(8,128)(2,1)S(1)}, bf16[2,4,2,2,8,768]{5,4,3,2,1,0:T(8,128)(2,1)}, u32[]{:S(2)}) copy-start(bf16[2,4,2,2,8,768]{5,4,3,2,1,0:T(8,128)(2,1)} %get-tuple-element.61) | copy-start | bytes 1179652
  573.0 21.9 %all-to-all-start = ((f32[32,8,72]{2,1,0:T(8,128)}), f32[32,8,72]{2,1,0:T(8,128)}, u32[]{:S(2)}, u32[]{:S(2)}) async-start(f32[32,8,72]{2,1,0:T(8,128)} %bitcast.20), calls=%async_computation | async-start | bytes 262144 | tf_op jit(solution)/shard_map/all_to_all | solution.py:1371
  578.0 4.8 copy-start.10
  578.7 6.0 copy-start.18
  578.7 6.0 copy-start.22
  578.7 6.0 copy-start.23
  578.7 6.6 %copy-start.4 = (f32[72,1728]{1,0:T(8,128)S(1)}, f32[72,1728]{1,0:T(8,128)}, u32[]{:S(2)}) copy-start(f32[72,1728]{1,0:T(8,128)} %param.29) | copy-start | bytes 1492996
  580.7 7.2 %copy-start.3 = (f32[72,2304]{1,0:T(8,128)S(1)}, f32[72,2304]{1,0:T(8,128)}, u32[]{:S(2)}) copy-start(f32[72,2304]{1,0:T(8,128)} %param.35) | copy-start | bytes 1990660
  581.6 6.3 %copy-start.11 = (f32[72,2304]{1,0:T(8,128)S(1)}, f32[72,2304]{1,0:T(8,128)}, u32[]{:S(2)}) copy-start(f32[72,2304]{1,0:T(8,128)} %param.37) | copy-start | bytes 1990660
  581.7 6.2 %copy-start.12 = (f32[72,2304]{1,0:T(8,128)S(1)}, f32[72,2304]{1,0:T(8,128)}, u32[]{:S(2)}) copy-start(f32[72,2304]{1,0:T(8,128)} %param.36) | copy-start | bytes 1990660
  581.8 6.2 %copy-start.13 = (f32[72,2304]{1,0:T(8,128)S(1)}, f32[72,2304]{1,0:T(8,128)}, u32[]{:S(2)}) copy-start(f32[72,2304]{1,0:T(8,128)} %get-tuple-element.94) | copy-start | bytes 1990660
  587.9 1.5 copy-start.2
  587.9 1.8 copy-start.7
  587.9 2.3 copy-start.8
  587.9 2.5 copy-start.9
  589.5 2.5 copy-start
  589.5 2.5 copy-start.5
  589.5 2.5 copy-start.6
  589.5 2.5 copy-start.14
  592.0 2.3 copy-start.21
  592.0 2.3 copy-start.24
  592.0 2.3 copy-start.25
  592.0 3.9 copy-start.17

commit v2 on v1

--- a/solution.py
+++ b/solution.py
@@ -326,11 +326,19 @@
     full = jnp.concatenate([part, jnp.zeros((n, LANES-HEAD), part.dtype)], axis=1)
     return jnp.where(lanes((n,LANES)) < HEAD, full, aug)
 
+def split3(v):
+    hi = v.astype(LOW).astype(WIDE)
+    mid = (v - hi).astype(LOW).astype(WIDE)
+    lo = v - hi - mid
+    return hi, mid, lo
+
+
 def attend_kernel(*refs):
     slots, x_ref, table, bias, weight, seg_ref, fc2_s = refs[:7]
-    act_turned, joint_ref, mixed_ref, turned_ref, lse_ref, proj_w, fc1_w, fc2_w = refs[9:17]
-    qh, kh, vh = refs[17:20]
-    *sems, local = refs[20:]
+    act_turned, mixed_ref, turned_ref = refs[9:12]
+    saved, (proj_w, fc1_w, fc2_w) = refs[12:16], refs[16:19]
+    heads, (*sems, local, save_sems) = refs[19:23], refs[23:]
+    qh, kh, vh, oh = heads
     proj, fc1, fc2 = (
         Gather(w, s, r) for w, s, r in zip((proj_w, fc1_w, fc2_w), sems[0::2], sems[1::2])
     )
@@ -348,19 +356,25 @@
         act = (h1 * (1.0 + row_of(table, slot, 1)) + row_of(table, slot, 0)).astype(LOW)
         act_turned[:, rows] = act.T
         joint = jnp.concatenate([times(act, weight[0]), times(act, weight[1])], axis=1)
-        joint_ref[rows, :] = (joint + bias[...]).astype(LOW)
+        joint = (joint + bias[...]).astype(LOW)
         lane = lanes((CHUNK, LANES))
         qc, kc = seg_codes(seg_ref[rows, :], CHUNK)
-        qc = qc.astype(LOW); kc = kc.astype(LOW)
+        qc = qc.astype(LOW)
+        kc = jnp.where(jnp.logical_and(lane >= HEAD + 4, lane < HEAD + 7), 1.0, kc).astype(LOW)
         ones = jnp.where(jnp.logical_and(lane >= HEAD, lane < HEAD+3), 1.0, 0.0).astype(LOW)
         for h in range(HEADS):
-            qh[h, rows, :] = pad_head(joint_ref[rows, h*HEAD:(h+1)*HEAD], qc)
-            kh[h, rows, :] = pad_head(joint_ref[rows, D+h*HEAD:D+(h+1)*HEAD], kc)
-            vh[h, rows, :] = pad_head(joint_ref[rows, 2*D+h*HEAD:2*D+(h+1)*HEAD], ones)
+            qh[h, rows, :] = pad_head(joint[:, h*HEAD:(h+1)*HEAD], qc)
+            kh[h, rows, :] = pad_head(joint[:, D+h*HEAD:D+(h+1)*HEAD], kc)
+            vh[h, rows, :] = pad_head(joint[:, 2*D+h*HEAD:2*D+(h+1)*HEAD], ones)
         pl.when(i == 2)(proj.cross)
         return carry
     lax.fori_loop(0, T//CHUNK, fill, 0)
-    lse_ref[...] = jnp.zeros_like(lse_ref)
+
+    def save(number):
+        return pltpu.make_async_copy(heads[number], saved[number], save_sems.at[number])
+
+    save(1).start()
+    save(2).start()
     def head(h, carry):
         k = kh[h]; v = vh[h]
         for i in range(T//CHUNK):
@@ -371,9 +385,12 @@
             p = jnp.exp2((s - m)*(HEAD**-0.5*LOG2E)).astype(LOW)
             o = jnp.dot(p, v, preferred_element_type=WIDE)
             l = o[:, HEAD:HEAD+1]
-            qh[h, rows, :] = (o / l).astype(LOW)
-            col = m*HEAD**-0.5 + jnp.log(l)
-            lse_ref[rows, :] = jnp.where(lanes((CHUNK,LANES)) == h, col, lse_ref[rows, :])
+            oh[h, rows, :] = (o / l).astype(LOW)
+            hi, mid, lo = split3(-(m + jnp.log(l) * HEAD**0.5))
+            lane = lanes((CHUNK, LANES))
+            q = jnp.where(lane == HEAD + 4, hi.astype(LOW), q)
+            q = jnp.where(lane == HEAD + 5, mid.astype(LOW), q)
+            qh[h, rows, :] = jnp.where(lane == HEAD + 6, lo.astype(LOW), q)
         tasks = {
             3: lambda: (fc2.finish_far(fc2_s, local.at[0]), fc2.spread()),
             6: fc1.cross,
@@ -388,9 +405,12 @@
 
         return carry
     lax.fori_loop(0, HEADS, head, 0)
+    save(0).start()
+    save(3).start()
+
     def drain(i, carry):
         rows = pl.ds(pl.multiple_of(i*CHUNK, CHUNK), CHUNK)
-        mixed = jnp.concatenate([qh[h, rows, :][:, :HEAD] for h in range(HEADS)], axis=1)
+        mixed = jnp.concatenate([oh[h, rows, :][:, :HEAD] for h in range(HEADS)], axis=1)
         mixed_ref[rows, :] = mixed
         turned_ref[:, rows] = mixed.T
         return carry
@@ -400,32 +420,39 @@
     fc1.end()
     fc2.close()
     fc2.end()
+    for number in range(4):
+        save(number).wait()
 
 
 def attend(slots, x_in, table, bias, weight, segments, fc2_s, proj_w, fc1_w):
     tokens = x_in.shape[0]
     wide = HEADS * HEAD
-    return pl.pallas_call(
+    heads = (HEADS, tokens, LANES)
+    out = pl.pallas_call(
         attend_kernel,
         out_shape=(
             jax.ShapeDtypeStruct((wide, tokens), LOW),
-            jax.ShapeDtypeStruct((tokens, 3 * wide), LOW),
             jax.ShapeDtypeStruct((tokens, wide), LOW),
             jax.ShapeDtypeStruct((wide, tokens), LOW),
-            jax.ShapeDtypeStruct((tokens, LANES), WIDE),
+        )
+        + (jax.ShapeDtypeStruct(heads, LOW),) * 4
+        + (
             jax.ShapeDtypeStruct(proj_w.shape, LOW),
             jax.ShapeDtypeStruct(fc1_w.shape, LOW),
             whole_shape(fc2_s),
         ),
         in_specs=[pl.BlockSpec(memory_space=pltpu.SMEM)] + [VMEM] * 6 + [ANY] * 2,
-        out_specs=(VMEM,) * 5 + (ANY,) * 3,
-        scratch_shapes=[pltpu.VMEM((HEADS, tokens, LANES), LOW)] * 3 + gather_scratch(3, 1),
-        input_output_aliases={7: 5, 8: 6},
+        out_specs=(VMEM,) * 3 + (ANY,) * 7,
+        scratch_shapes=[pltpu.VMEM(heads, LOW)] * 4
+        + gather_scratch(3, 1)
+        + [pltpu.SemaphoreType.DMA((4,))],
+        input_output_aliases={7: 7, 8: 8},
         compiler_params=pltpu.CompilerParams(
             collective_id=1, has_side_effects=True, vmem_limit_bytes=60 * 2**20
         ),
         name="attend",
     )(slots, x_in, table, bias, weight, segments.reshape(tokens, 1), fc2_s, proj_w, fc1_w)
+    return out[0], out[1], out[2], out[3:7], out[7:]
 
 
 def row_spans(rows):
@@ -509,6 +536,38 @@
         self._first().wait_send()
         self._second().wait_send()
 
+    def early(self):
+        second = self.part(self.second)
+        self._both().wait_recv()
+        self._first().wait_recv()
+
+        def add(at, carry):
+            self.joint[at] = (second[at].astype(WIDE) + self.came_both[at].astype(WIDE)).astype(LOW)
+            self.total_[at] = (self.base[at].astype(WIDE) + self.came_first[at].astype(WIDE)).astype(LOW)
+            return carry
+
+        lax.fori_loop(0, self.count, add, 0)
+        self._both().wait_send()
+        self._first().wait_send()
+
+    def _load_base(self):
+        return pltpu.make_async_copy(self.base, self.total_, self.locals_.at[1])
+
+    def late_start(self):
+        self._load_base().start()
+        self._second().start()
+
+    def late_total(self):
+        self._load_base().wait()
+        self._second().wait_recv()
+
+        def add(at, carry):
+            self.total_[at] = (self.total_[at].astype(WIDE) + self.came_second[at].astype(WIDE)).astype(LOW)
+            return carry
+
+        lax.fori_loop(0, self.count, add, 0)
+        self._second().wait_send()
+
     def start_far(self):
         for distance in range(1, self.count):
             self._far(distance).start()
@@ -560,7 +619,7 @@
     count, rows, columns = shape[2:]
     shapes = []
     for span in row_spans(rows):
-        shapes += came_scratch(count, span, columns)
+        shapes += came_scratch(count, span, columns, total)
         shapes += [pltpu.VMEM((count, span[1], columns), LOW)] * (2 if total else 1)
         shapes += sem_scratch(count)
     return shapes
@@ -569,7 +628,8 @@
 def loaded_reduces(sums, scratch, totals=None):
     reduces = []
     for number, span in enumerate(row_spans(sums.shape[3])):
-        came, scratch = take(scratch, 4)
+        came, scratch = take(scratch, 4 if totals is None else 3)
+        came = list(came) + [None] * (4 - len(came))
         (joint,), scratch = take(scratch, 1)
         if totals is None:
             (total,), scratch = take(scratch, 1)
@@ -590,18 +650,46 @@
     return shapes
 
 
-def resident_reduces(sums, scratch, totals=None):
+def resident_reduces(sums, scratch, totals=None, joints=None):
     reduces = []
     for number, span in enumerate(row_spans(sums.shape[3])):
-        came, scratch = take(scratch, 4 if totals is None else 3)
+        came, scratch = take(scratch, 4 if totals is None else 3 if joints is None else 2)
         sems, scratch = take(scratch, 3)
         part = span_part(sums, span)
         order = ORDERS[number]
         own = part()
         total = own if totals is None else totals[number]
         came = list(came) + [None] * (4 - len(came))
-        joint = part("near" if order == "mod" else "mod")
+        joint = part("near" if order == "mod" else "mod") if joints is None else joints[number]
         reduces.append(Reduce(part, span, order, came, joint, total, own, sems))
+    return reduces, scratch
+
+
+def early_scratch(shape):
+    count, rows, columns = shape[2:]
+    shapes = []
+    for span in row_spans(rows):
+        shapes += [pltpu.VMEM((count, span[1], columns), LOW)] * 2 + sem_scratch(count)
+    return shapes
+
+
+def late_scratch(bases):
+    shapes = []
+    for base in bases:
+        far = pltpu.VMEM((base.shape[0] - 1,) + base.shape[1:], LOW)
+        shapes += [pltpu.VMEM(base.shape, LOW)] * 2 + [far] + sem_scratch(base.shape[0])
+    return shapes
+
+
+def late_reduces(joints, bases, rows, scratch):
+    reduces = []
+    for number, span in enumerate(row_spans(rows)):
+        (came, total, came_far), scratch = take(scratch, 3)
+        sems, scratch = take(scratch, 3)
+        came = (None, None, came, came_far)
+        reduces.append(
+            Reduce(None, span, ORDERS[number], came, joints[number], total, bases[number], sems)
+        )
     return reduces, scratch
 
 
@@ -632,19 +720,17 @@
     def scratch(count, rows, tokens, columns):
         sums = pltpu.VMEM((2, 2, count, rows, columns), LOW)
         sems = [pltpu.SemaphoreType.DMA((4,))] * 3
-        return [pltpu.VMEM((4, count, rows, tokens), LOW), sums, sums] + sems
+        return [pltpu.VMEM((2, count, rows, tokens), LOW), sums, sums] + sems
 
     def _load(self, near, own):
         core = self.core if own else 1 - self.core
-        slot = 2 * own + near
         return pltpu.make_async_copy(
-            self.left.at[:, near, core], self.rows_.at[slot], self.loads.at[slot]
+            self.left.at[:, near, core], self.rows_.at[near], self.loads.at[2 * own + near]
         )
 
     def load(self):
-        for own in (0, 1):
-            for near in (0, 1):
-                self._load(near, own).start()
+        for near in (0, 1):
+            self._load(near, 0).start()
 
     def _copy(self, mod, near):
         return remote(
@@ -660,7 +746,7 @@
         count, rows, tokens = self.rows_.shape[1:]
         columns = self.right.shape[2]
         self._load(near, own).wait()
-        left = self.rows_[2 * own + near].reshape(count * rows, tokens)
+        left = self.rows_[near].reshape(count * rows, tokens)
         width = columns if columns <= 1024 else columns // 2
         width = width if width % LANES == 0 else columns
         for mod in (0, 1):
@@ -675,6 +761,7 @@
                 self.sums[mod, near, :, :, at : at + width] = product.astype(LOW)
 
             self._blocks(near, 0, store)
+            self._load(near, 1).start()
             for mod in (0, 1):
                 self._copy(mod, near).start()
 
@@ -695,76 +782,90 @@
     return [jax.ShapeDtypeStruct((count, span[1], columns), LOW) for span in row_spans(rows)]
 
 
-def weight_kernel(*refs, spans, stored):
-    count = stored + (spans > 0)
-    sides, refs = take(refs, 2 * count)
-    outs, refs = take(refs, stored)
-    totals, scratch = take(refs, spans)
-    products = []
-    for number in range(count):
+def weight_kernel(*refs, modes, spans):
+    sides, refs = take(refs, 2 * len(modes))
+    outs = []
+    for mode, count in zip(modes, spans):
+        used, refs = take(refs, {"whole": count, "early": 2 * count, "chip": 1}[mode])
+        outs.append(used)
+    scratch = refs
+    products, reduces = [], []
+    for number in range(len(modes)):
         used, scratch = take(scratch, 6)
         products.append(Product(sides[2 * number], sides[2 * number + 1], used))
-    reduces = []
-    if spans:
-        reduces, scratch = resident_reduces(products[0].sums, scratch, totals)
-    (out_sems,) = scratch
+    for mode, count, product, out in zip(modes, spans, products, outs):
+        parts = []
+        if mode == "whole":
+            parts, scratch = resident_reduces(product.sums, scratch, out)
+        elif mode == "early":
+            parts, scratch = resident_reduces(product.sums, scratch, out[count:], out[:count])
+        reduces.append(parts)
+    (out_sem,) = scratch
     products[0].load()
     greet()
     copies = []
     for number, product in enumerate(products):
+        before = number and modes[number - 1] == "whole"
         product.send()
-        if number + 1 < count:
+        if before:
+            run(reduces[number - 1], "merge")
+        if number + 1 < len(products):
             products[number + 1].load()
         product.sum()
-        if spans and number == 0:
-            run(reduces, "start")
-            continue
-        copy = pltpu.make_async_copy(product.sums, outs[len(copies)], out_sems.at[len(copies)])
-        copy.start()
-        copies.append(copy)
-        if spans and number == 1:
-            run(reduces, "merge")
-    if spans and count == 1:
-        run(reduces, "merge")
-    run(reduces, "total")
+        run(reduces[number], "start") if reduces[number] else None
+        if before:
+            run(reduces[number - 1], "total")
+        if modes[number] == "chip":
+            copies.append(pltpu.make_async_copy(product.sums, outs[number][0], out_sem.at[0]))
+            copies[-1].start()
+    for number, mode in enumerate(modes):
+        if mode == "early":
+            run(reduces[number], "early")
     for copy in copies:
         copy.wait()
 
 
-def weight_call(summed, stored, number):
-    pairs = summed + stored
-    count, _, _, rows, tokens = pairs[0][0].shape
-    columns = pairs[0][1].shape[2]
-    totals = total_shapes(count, rows, columns) if summed else []
-    scratch = []
-    for left, right in pairs:
-        scratch += Product.scratch(count, left.shape[3], tokens, right.shape[2])
-    if summed:
-        scratch += resident_scratch((2, 2, count, rows, columns), False)
+def weight_call(pairs, modes, number):
+    count = pairs[0][0].shape[0]
+    tokens = pairs[0][0].shape[4]
+    products, sums, shapes, specs, spans = [], [], [], [], []
+    for (left, right), mode in zip(pairs, modes):
+        rows, columns = left.shape[3], right.shape[2]
+        shape = (2, 2, count, rows, columns)
+        products += Product.scratch(count, rows, tokens, columns)
+        totals = total_shapes(count, rows, columns)
+        spans.append(len(totals))
+        if mode == "chip":
+            shapes.append(jax.ShapeDtypeStruct(shape, LOW))
+            specs.append(ANY)
+        else:
+            sums += resident_scratch(shape, False) if mode == "whole" else early_scratch(shape)
+            outs = totals * (1 if mode == "whole" else 2)
+            shapes += outs
+            specs += [VMEM] * len(outs)
     out = pl.pallas_call(
-        partial(weight_kernel, spans=len(totals), stored=len(stored)),
-        out_shape=tuple(
-            jax.ShapeDtypeStruct((2, 2, count, left.shape[3], right.shape[2]), LOW) for left, right in stored
-        )
-        + tuple(totals),
+        partial(weight_kernel, modes=modes, spans=tuple(spans)),
+        out_shape=tuple(shapes),
         in_specs=[ANY, VMEM] * len(pairs),
-        out_specs=(ANY,) * len(stored) + (VMEM,) * len(totals),
-        scratch_shapes=scratch + [pltpu.SemaphoreType.DMA((2,))],
+        out_specs=tuple(specs),
+        scratch_shapes=products + sums + [pltpu.SemaphoreType.DMA((1,))],
         compiler_params=pltpu.CompilerParams(
             collective_id=number, has_side_effects=True, vmem_limit_bytes=63 * 2**20
         ),
         name="weight_grads",
     )(*[side for pair in pairs for side in pair])
-    return out[: len(stored)], out[len(stored) :]
+    return out, spans
 
 
 def weight_grads(hidden, branch, mlp, pre, mixed, attn):
-    summed, stored = [(hidden, branch)], [(mlp, pre), (mixed, attn)]
+    proj, fc2, fc1 = (mixed, attn), (hidden, branch), (mlp, pre)
     if mlp.shape[3] % 8 == 0:
-        return weight_call(summed, stored, 4)
-    _, totals = weight_call(summed, [], 4)
-    sums, _ = weight_call([], stored, 5)
-    return sums, totals
+        out, spans = weight_call([proj, fc2, fc1], ("whole", "early", "chip"), 4)
+        first, second = spans[0], spans[0] + spans[1]
+        return out[:first], out[first:second], out[second:-1], out[-1]
+    early, spans = weight_call([fc2], ("early",), 4)
+    rest, _ = weight_call([proj, fc1], ("whole", "chip"), 5)
+    return rest[:-1], early[: spans[0]], early[spans[0] :], rest[-1]
 
 
 def tile_sums_by_slot(chooser, sums):
@@ -882,73 +983,50 @@
     )(slots, act, joint, x_in, dx1, table, weight, mid_sums, pre_sums, chooser, *totals)
 
 
-def split3(v):
-    hi = v.astype(LOW).astype(WIDE)
-    mid = (v - hi).astype(LOW).astype(WIDE)
-    lo = v - hi - mid
-    return hi, mid, lo
-
-
-def attend_back_kernel(*refs, fc2_spans, spans):
-    qkv_ref, seg_ref, mixed_ref, lse_ref, up_ref, fc1_sums, proj_sums = refs[:7]
-    fc2_totals, refs = take(refs[7:], fc2_spans)
+def attend_back_kernel(*refs, counts):
+    up_ref, heads, fc1_sums = refs[0], refs[1:5], refs[5]
+    proj_totals, refs = take(refs[6:], counts[0])
+    joints, refs = take(refs, counts[1])
+    bases, refs = take(refs, counts[1])
     out_ref, fc2_out, proj_out, *refs = refs
-    fc1_totals, refs = take(refs, spans)
-    qh, kh, vh, uh, stage, stage_sems, leave, leave_sems, *scratch = refs
-    proj, scratch = loaded_reduces(proj_sums, scratch)
+    fc1_totals, refs = take(refs, counts[2])
+    qh, kh, vh, uh, oh, load_sems, leave, leave_sems, *scratch = refs
     fc1, scratch = loaded_reduces(fc1_sums, scratch, fc1_totals)
-    fc2, scratch = far_reduces(fc2_totals, fc2_out.shape[0], scratch)
-    T = mixed_ref.shape[0]
+    proj, scratch = far_reduces(proj_totals, proj_out.shape[0], scratch)
+    fc2, scratch = late_reduces(joints, bases, fc2_out.shape[0], scratch)
+    T = up_ref.shape[0]
     chunks = T // CHUNK
+
+    def load(number):
+        return pltpu.make_async_copy(heads[number], (qh, kh, vh, oh)[number], load_sems.at[number])
+
+    for number in (3, 0, 1, 2):
+        load(number).start()
     greet()
-    run(fc2, "start_far")
+    run(fc2, "late_start")
+    run(proj, "start_far")
     run(fc1, "start")
-
-    def load(i):
-        rows = pl.ds(pl.multiple_of(i * CHUNK, CHUNK), CHUNK)
-        slot = lax.rem(i, 2)
-        return pltpu.make_async_copy(qkv_ref.at[rows], stage.at[slot], stage_sems.at[slot])
-
-    load(0).start()
+    load(3).wait()
 
     def fill(i, carry):
         rows = pl.ds(pl.multiple_of(i * CHUNK, CHUNK), CHUNK)
-
-        @pl.when(i + 1 < chunks)
-        def _():
-            load(i + 1).start()
-
-        load(i).wait()
-        qkv = stage.at[lax.rem(i, 2)]
         lane = lanes((CHUNK, LANES))
-        qc, kc = seg_codes(seg_ref[rows, :], CHUNK)
-        kc = jnp.where(jnp.logical_and(lane >= HEAD + 4, lane < HEAD + 7), 1.0, kc).astype(LOW)
-        ones = jnp.where(jnp.logical_and(lane >= HEAD, lane < HEAD + 3), 1.0, 0.0).astype(LOW)
-
-        def spread(v, at, base):
-            hi, mid, lo = split3(v)
-            return jnp.where(
-                lane == at, hi, jnp.where(lane == at + 1, mid, jnp.where(lane == at + 2, lo, base))
-            )
-
         for h in range(HEADS):
-            a, b = h * HEAD, (h + 1) * HEAD
-            qa = spread(-lse_ref[rows, h : h + 1] * HEAD**0.5, HEAD + 4, qc).astype(LOW)
-            qh[h, rows, :] = pad_head(qkv[:, a:b], qa)
-            kh[h, rows, :] = pad_head(qkv[:, D + a : D + b], kc)
-            vh[h, rows, :] = pad_head(qkv[:, 2 * D + a : 2 * D + b], ones)
-            u = up_ref[rows, a:b]
-            delta = jnp.sum(u.astype(WIDE) * mixed_ref[rows, a:b].astype(WIDE), axis=1, keepdims=True)
-            ua = spread(-delta, HEAD, jnp.zeros((CHUNK, LANES), WIDE)).astype(LOW)
-            uh[h, rows, :] = pad_head(u, ua)
+            u = pad_head(up_ref[rows, h * HEAD : (h + 1) * HEAD], jnp.zeros((CHUNK, LANES), LOW))
+            delta = jnp.sum(u.astype(WIDE) * oh[h, rows, :].astype(WIDE), axis=1, keepdims=True)
+            hi, mid, lo = split3(-delta)
+            u = jnp.where(lane == HEAD, hi.astype(LOW), u)
+            u = jnp.where(lane == HEAD + 1, mid.astype(LOW), u)
+            uh[h, rows, :] = jnp.where(lane == HEAD + 2, lo.astype(LOW), u)
         return carry
 
     lax.fori_loop(0, chunks, fill, 0)
+    for number in range(3):
+        load(number).wait()
     across = (((1,), (1,)), ((), ()))
     tasks = {
-        4: lambda: (run(fc1, "merge"), run(proj, "start")),
-        11: lambda: run(proj, "merge"),
-        14: lambda: run(proj, "total", "start_far"),
+        4: lambda: run(fc2, "late_total", "start_far"),
+        9: lambda: run(fc1, "merge"),
     }
 
     def head(h, carry):
@@ -1011,32 +1089,35 @@
         part.final(proj_out)
 
 
-def attend_back(qkv, segments, mixed, lse, upstream, fc1_sums, proj_sums, fc2_totals):
-    tokens = qkv.shape[0]
+def attend_back(upstream, heads, fc1_sums, proj_totals, joints, bases):
+    tokens = upstream.shape[0]
     count, rows, columns = fc1_sums.shape[2:]
     totals = total_shapes(count, rows, columns)
-    fc2_rows = sum(total.shape[1] for total in fc2_totals)
+
+    def shard(parts):
+        return jax.ShapeDtypeStruct((sum(part.shape[1] for part in parts), parts[0].shape[2]), WIDE)
+
     out = pl.pallas_call(
-        partial(attend_back_kernel, fc2_spans=len(fc2_totals), spans=len(totals)),
+        partial(attend_back_kernel, counts=(len(proj_totals), len(joints), len(totals))),
         out_shape=(
             jax.ShapeDtypeStruct((2, tokens, 3 * HEADS * HEAD // 2), LOW),
-            jax.ShapeDtypeStruct((fc2_rows, fc2_totals[0].shape[2]), WIDE),
-            jax.ShapeDtypeStruct(proj_sums.shape[3:], WIDE),
+            shard(bases),
+            shard(proj_totals),
         )
         + tuple(totals),
-        in_specs=[ANY] + [VMEM] * 4 + [ANY] * 2 + [VMEM] * len(fc2_totals),
+        in_specs=[VMEM] + [ANY] * 5 + [VMEM] * len(proj_totals) + [ANY] * (2 * len(joints)),
         out_specs=(ANY, VMEM, VMEM) + (VMEM,) * len(totals),
-        scratch_shapes=[pltpu.VMEM((HEADS, tokens, LANES), LOW)] * 4
-        + [pltpu.VMEM((2, CHUNK, 3 * HEADS * HEAD), LOW), pltpu.SemaphoreType.DMA((2,))]
+        scratch_shapes=[pltpu.VMEM((HEADS, tokens, LANES), LOW)] * 5
+        + [pltpu.SemaphoreType.DMA((4,))]
         + [pltpu.VMEM((2, CHUNK, 3 * HEADS * HEAD // 2), LOW), pltpu.SemaphoreType.DMA((2,))]
-        + loaded_scratch(proj_sums.shape)
         + loaded_scratch(fc1_sums.shape, False)
-        + far_scratch(fc2_totals),
+        + far_scratch(proj_totals)
+        + late_scratch(bases),
         compiler_params=pltpu.CompilerParams(
             collective_id=2, has_side_effects=True, vmem_limit_bytes=63 * 2**20
         ),
         name="attend_back",
-    )(qkv, segments.reshape(tokens, 1), mixed, lse, upstream, fc1_sums, proj_sums, *fc2_totals)
+    )(upstream, *heads, fc1_sums, *proj_totals, *joints, *bases)
     return out[0], out[1], out[2], out[3:]
 
 
@@ -1301,7 +1382,7 @@
     def blocked(turned):
         return turned.reshape(row_devices // 4, 2, 2, -1, tokens)
 
-    act_turned, joint_rows, mixture, mixture_turned, log_totals, proj_w, fc1_w, fc2_w = attend(
+    act_turned, mixture, mixture_turned, heads, (proj_w, fc1_w, fc2_w) = attend(
         slots,
         x_in,
         table,
@@ -1317,7 +1398,7 @@
     ) = middle(
         slots, x_in, out_grad, mixture, table, bias_full, joined(proj_w), joined(fc1_w), joined(fc2_w)
     )
-    (fc1_sums, proj_sums), fc2_totals = weight_grads(
+    proj_totals, fc2_joints, fc2_bases, fc1_sums = weight_grads(
         blocked(hidden_turned),
         branch_halves,
         blocked(mlp_turned),
@@ -1326,14 +1407,7 @@
         attn_halves,
     )
     joint_halves, fc2_shard, proj_shard, fc1_totals = attend_back(
-        joint_rows,
-        segments,
-        mixture,
-        log_totals,
-        mixture_grad,
-        fc1_sums,
-        proj_sums,
-        fc2_totals,
+        mixture_grad, heads, fc1_sums, proj_totals, fc2_joints, fc2_bases
     )
     chooser = (slots[None, :] == (jnp.arange(2 * images, dtype=jnp.int32) % images)[:, None]).astype(WIDE)
     qkv_shard, fc1_shard, small_grads, x_grad = last_scatter(

time: 609 us -> 584 us (0.959)
  Pallas kernels: 552 us -> 525 us
    pallas_call x2, Pallas kernels: 159 us -> 135 us  [the longest x1 68 us: attend_back(): pl.pallas_call(partial(attend_back_kernel, counts=(len(proj_totals), len(...]
where the time goes in v2:
time: 584 us; the launch traced here: 577 us
  Pallas kernels  525 us (90%)
  other arithmetic  23.9 us (4%)
  local copies, waits for them, and re-layouts  18.3 us (3%)
    pallas_call x1, Pallas kernels, attend(): pl.pallas_call(attend_kernel, out_shape=(jax.ShapeDtypeStruct((wide, toke...  127 us
    pallas_call x1, Pallas kernels, middle(): pl.pallas_call(middle_kernel, out_shape=tuple((jax.ShapeDtypeStruct(shape...  98.9 us
    pallas_call x1, Pallas kernels, first_gather(): pl.pallas_call(first_kernel, out_shape=tuple((whole_shape(shard) for shar...  83.5 us
    pallas_call x1, Pallas kernels, last_scatter(): pl.pallas_call(partial(last_kernel, spans=len(totals)), out_shape=(jax.Sh...  81.1 us
    pallas_call x1, Pallas kernels, attend_back(): pl.pallas_call(partial(attend_back_kernel, counts=(len(proj_totals), len(...  68 us
    pallas_call x1, Pallas kernels, weight_call(): pl.pallas_call(partial(weight_kernel, modes=modes, spans=tuple(spans)), o...  67.1 us
  transfers between devices with their start and end apart: 1, of which 0 were waited for; matrix products, arithmetic and copies ran while one was open for 3% of the time, Pallas kernels for 0%

profile of v2, /device:TPU:0, one launch (start us, length us, event | category | flops | bytes accessed | tf_op | source)
XLA Modules:
  0.0 576.6 jit_solution(10135670450536026766)
XLA Ops:
  0.7 0.7 convert_element_type.49
  1.4 0.7 convert_element_type.54
  2.1 0.7 fusion.8
  2.8 0.1 reshape.151
  3.0 1.6 convert_element_type.51.refs_2_
  4.6 1.8 convert_element_type.50.refs_1_
  6.4 1.9 convert_element_type.52.refs_3_
  8.2 1.3 convert_element_type.53
  9.6 0.2 dynamic_update_slice.3
  9.8 1.0 fusion.2.refs_4_
  10.8 0.7 maximum_maximum_fusion.refs_0_
  11.4 83.5 %first_gather.1 = (bf16[2,4,2,2,8,768]{5,4,3,2,1,0:T(8,128)(2,1)}, bf16[2,4,2,2,72,1728]{5,4,3,2,1,0:T(8,128)(2,1)}, bf16[2,4,2,2,72,576]{5,4,3,2,1,0:T(8,128)(2...) custom-call(bf16[8,768]{1,0:T(8,128)(2,1)} %maximum_maximum_fusion.refs_0_, ...), custom_call_target="tpu_custom_call" | custom-call | tf_op jit(solution)/shard_map/first_gather/pallas_call | solution.py:286
  95.0 1.0 slice.36
  96.1 0.1 reshape.173.bias
  96.2 0.6 slice.40
  96.9 0.8 convert_element_type.58.refs_6_
  97.7 1.0 copy.63.refs_5_
  98.7 0.7 compare_convert_fusion.refs_9_
  99.4 1.6 constant_dynamic-slice_fusion.1
  101.0 0.6 fusion.14.refs_3_
  101.6 126.6 %attend.1 = (bf16[1152,1024]{1,0:T(8,128)(2,1)}, bf16[1024,1152]{1,0:T(8,128)(2,1)}, bf16[1152,1024]{1,0:T(8,128)(2,1)}, bf16[16,1024,128]{2,1,0:T(8,128)(2,1)},...) custom-call(s32[4]{0:T(128)} %copy-done.18, ...), custom_call_target="tpu_custom_call", output_to_operand_aliasing={{7}: (7, {}), {8}: (8, {})} | custom-call | tf_op jit(solution)/shard_map/attend/pallas_call | solution.py:431
  228.2 98.9 %middle.1 = (bf16[1024,1152]{1,0:T(8,128)(2,1)}, bf16[1152,1024]{1,0:T(8,128)(2,1)}, bf16[4608,1024]{1,0:T(8,128)(2,1)}, bf16[2,1024,2304]{2,1,0:T(8,128)(2,1)},...) custom-call(s32[4]{0:T(128)} %copy-done.18, ...), custom_call_target="tpu_custom_call" | custom-call | flops 48922361856 | bytes 71073792 | tf_op jit(solution)/shard_map/middle/pallas_call | solution.py:1268
  327.1 67.1 %weight_grads.1 = (bf16[4,40,576]{2,1,0:T(8,128)(2,1)}, bf16[4,32,576]{2,1,0:T(8,128)(2,1)}, bf16[4,144,576]{2,1,0:T(8,128)(2,1)}, bf16[4,144,576]{2,1,0:T(8,128...) custom-call(bf16[4,2,2,72,1024]{4,3,2,1,0:T(8,128)(2,1)} %bitcast.49, ...), custom_call_target="tpu_custom_call" | custom-call | tf_op jit(solution)/shard_map/weight_grads/pallas_call | solution.py:846
  394.2 68.0 %attend_back.1 = (bf16[2,1024,1728]{2,1,0:T(8,128)(2,1)}, f32[288,576]{1,0:T(8,128)}, f32[72,576]{1,0:T(8,128)}, bf16[4,40,2304]{2,1,0:T(8,128)(2,1)}, bf16[4,32,2304]{2,1,0:T(8,128)(2,1)}) custom-call(bf16[1024,1152]{1,0:T(8,128)(2,1)} %get-tuple-element.76.refs_0_, bf16[16,1024,128]{2,1,0:T(8,128)(2,1)} %get-tuple-element.77.refs_1_, ...), custom_call_target="tpu_custom_call" | custom-call | tf_op jit(solution)/shard_map/attend_back/pallas_call | solution.py:1100
  462.2 81.1 %last_scatter.1 = (f32[72,1728]{1,0:T(8,128)}, f32[72,2304]{1,0:T(8,128)}, bf16[2,4,2,2,16,3456]{5,4,3,2,1,0:T(8,128)(2,1)}, f32[1024,1152]{1,0:T(8,128)}) custom-call(s32[4]{0:T(128)} %copy-done.18, bf16[4,2,2,72,1024]{4,3,2,1,0:T(8,128)(2,1)} %bitcast.48, bf16[2,1024,1728]{2,1,0:T(8,128)(2,1)} %get-tuple-element.94.refs_2_, bf16[1024,1152]{1,0:T(8,128)(2,1)} %refs_3_.1, ...), custom_call_target="tpu_custom_call" | custom-call | tf_op jit(solution)/shard_map/last_scatter/pallas_call | solution.py:960
  543.3 1.9 copy_bitcast_fusion
  545.2 0.2 reshape.167
  545.5 0.4 fusion.3
  545.9 0.7 broadcast_in_dim.19
  546.5 5.1 all-to-all-start
  551.7 1.7 slice_bitcast_fusion
  553.4 1.7 slice.41
  555.1 0.2 reshape.171
  555.3 0.9 copy.68
  556.3 0.1 convert_reduce_fusion
  556.4 1.0 convert_reduce_fusion.1
  557.4 1.9 add_multiply_fusion.4
  559.3 0.6 add_multiply_fusion.5
  559.9 2.8 add_multiply_fusion.3
  562.7 1.5 add_multiply_fusion.2
  564.3 1.5 add_multiply_fusion.1
  565.8 0.7 copy-done.5
  566.5 0.3 copy-done.6
  566.8 2.2 add_multiply_fusion
  569.1 0.6 add_multiply_fusion.6
  569.7 0.9 bitcast_reduce_fusion
  570.7 0.6 fusion.10
  571.4 4.8 copy.76
  (65 shorter events, 0.5 us)
Async XLA Ops:
  3.0 93.9 %copy-start.19 = (s32[1024]{0:T(1024)S(1)}, s32[1024]{0:T(1024)}, u32[]{:S(2)}) copy-start(s32[1024]{0:T(1024)} %param.27) | copy-start | bytes 12292
  3.0 94.0 %copy-start.1 = (f32[288,576]{1,0:T(8,128)S(1)}, f32[288,576]{1,0:T(8,128)}, u32[]{:S(2)}) copy-start(f32[288,576]{1,0:T(8,128)} %param.38) | copy-start | bytes 1990660
  96.2 132.0 %copy-start.15 = (f32[1,9216]{1,0:T(1,128)}, f32[1,9216]{1,0:T(1,128)S(1)}, u32[]{:S(2)}) copy-start(f32[1,9216]{1,0:T(1,128)S(1)} %reshape.173.bias) | copy-start | bytes 110596
  96.9 4.7 copy-start.18
  545.5 11.9 %copy-start.10 = (f32[72,576]{1,0:T(8,128)S(1)}, f32[72,576]{1,0:T(8,128)}, u32[]{:S(2)}) copy-start(f32[72,576]{1,0:T(8,128)} %param.32) | copy-start | bytes 497668
  546.5 23.1 %all-to-all-start = ((f32[32,8,72]{2,1,0:T(8,128)}), f32[32,8,72]{2,1,0:T(8,128)}, u32[]{:S(2)}, u32[]{:S(2)}) async-start(f32[32,8,72]{2,1,0:T(8,128)} %bitcast.20), calls=%async_computation | async-start | bytes 262144 | tf_op jit(solution)/shard_map/all_to_all | solution.py:1445
  551.6 7.7 %copy-start.17 = (f32[288]{0:T(512)S(1)}, f32[288]{0:T(512)}, u32[]{:S(2)}) copy-start(f32[288]{0:T(512)} %param.41) | copy-start | bytes 3460
  551.6 7.7 %copy-start.21 = (f32[288]{0:T(512)S(1)}, f32[288]{0:T(512)}, u32[]{:S(2)}) copy-start(f32[288]{0:T(512)} %param.43) | copy-start | bytes 3460
  551.6 7.7 %copy-start.22 = (f32[288]{0:T(512)S(1)}, f32[288]{0:T(512)}, u32[]{:S(2)}) copy-start(f32[288]{0:T(512)} %param.42) | copy-start | bytes 3460
  551.6 8.3 %copy-start.4 = (f32[72,1728]{1,0:T(8,128)S(1)}, f32[72,1728]{1,0:T(8,128)}, u32[]{:S(2)}) copy-start(f32[72,1728]{1,0:T(8,128)} %param.29) | copy-start | bytes 1492996
  555.3 7.4 %copy-start.3 = (f32[72,2304]{1,0:T(8,128)S(1)}, f32[72,2304]{1,0:T(8,128)}, u32[]{:S(2)}) copy-start(f32[72,2304]{1,0:T(8,128)} %param.35) | copy-start | bytes 1990660
  556.3 6.5 %copy-start.11 = (f32[72,2304]{1,0:T(8,128)S(1)}, f32[72,2304]{1,0:T(8,128)}, u32[]{:S(2)}) copy-start(f32[72,2304]{1,0:T(8,128)} %param.37) | copy-start | bytes 1990660
  556.4 6.4 %copy-start.12 = (f32[72,2304]{1,0:T(8,128)S(1)}, f32[72,2304]{1,0:T(8,128)}, u32[]{:S(2)}) copy-start(f32[72,2304]{1,0:T(8,128)} %param.36) | copy-start | bytes 1990660
  556.4 6.3 %copy-start.13 = (f32[72,2304]{1,0:T(8,128)S(1)}, f32[72,2304]{1,0:T(8,128)}, u32[]{:S(2)}) copy-start(f32[72,2304]{1,0:T(8,128)} %get-tuple-element.104) | copy-start | bytes 1990660
  559.9 4.3 copy-start.2
  559.9 4.3 copy-start.7
  559.9 4.3 copy-start.8
  559.9 4.3 copy-start.9
  564.2 1.6 copy-start
  564.2 2.3 copy-start.5
  564.2 2.6 copy-start.6
  564.2 2.6 copy-start.14
  566.8 2.3 copy-start.20
  566.8 2.3 copy-start.23
  566.8 2.3 copy-start.24
  566.8 3.9 copy-start.16

commit v3 on v2

--- a/solution.py
+++ b/solution.py
@@ -63,6 +63,13 @@
     for other in others:
         pl.semaphore_signal(barrier, inc=1, device_id=other, device_id_type=MESH)
     pl.semaphore_wait(barrier, len(others))
+
+
+def fetches(pairs, sems):
+    return [
+        pltpu.make_async_copy(source, target, sems.at[number])
+        for number, (source, target) in enumerate(pairs)
+    ]
 
 
 def remote(source, target, sends, receives, slot, other):
@@ -257,6 +264,7 @@
     greet()
     small.start_far(small_s, local.at[3])
     qkv.start_far(qkv_s, local.at[0])
+    proj.start_far(proj_s, local.at[1])
     small.finish_far(small_s, local.at[3])
     small.spread()
     small.cross()
@@ -267,7 +275,6 @@
     qkv.finish_far(qkv_s, local.at[0])
     qkv.spread()
     next(stages)
-    proj.start_far(proj_s, local.at[1])
     fc1.start_far(fc1_s, local.at[2])
     next(stages)
     qkv.cross()
@@ -334,10 +341,10 @@
 
 
 def attend_kernel(*refs):
-    slots, x_ref, table, bias, weight, seg_ref, fc2_s = refs[:7]
+    slots, x_hbm, table, bias, weight_hbm, seg_ref, fc2_s = refs[:7]
     act_turned, mixed_ref, turned_ref = refs[9:12]
     saved, (proj_w, fc1_w, fc2_w) = refs[12:16], refs[16:19]
-    heads, (*sems, local, save_sems) = refs[19:23], refs[23:]
+    heads, (x_ref, weight, fetch_sems, *sems, local, save_sems) = refs[19:23], refs[23:]
     qh, kh, vh, oh = heads
     proj, fc1, fc2 = (
         Gather(w, s, r) for w, s, r in zip((proj_w, fc1_w, fc2_w), sems[0::2], sems[1::2])
@@ -346,6 +353,11 @@
     fc2.start_far(fc2_s, local.at[0])
     proj.spread()
     fc1.spread()
+    loads = fetches(((x_hbm, x_ref), (weight_hbm, weight)), fetch_sems)
+    for load in loads:
+        load.start()
+    for load in loads:
+        load.wait()
 
     T = x_ref.shape[0]
 
@@ -441,9 +453,10 @@
             jax.ShapeDtypeStruct(fc1_w.shape, LOW),
             whole_shape(fc2_s),
         ),
-        in_specs=[pl.BlockSpec(memory_space=pltpu.SMEM)] + [VMEM] * 6 + [ANY] * 2,
+        in_specs=[pl.BlockSpec(memory_space=pltpu.SMEM), ANY, VMEM, VMEM, ANY, VMEM, VMEM, ANY, ANY],
         out_specs=(VMEM,) * 3 + (ANY,) * 7,
         scratch_shapes=[pltpu.VMEM(heads, LOW)] * 4
+        + [pltpu.VMEM(x_in.shape, LOW), pltpu.VMEM(weight.shape, LOW), pltpu.SemaphoreType.DMA((2,))]
         + gather_scratch(3, 1)
         + [pltpu.SemaphoreType.DMA((4,))],
         input_output_aliases={7: 7, 8: 8},
@@ -788,11 +801,14 @@
     for mode, count in zip(modes, spans):
         used, refs = take(refs, {"whole": count, "early": 2 * count, "chip": 1}[mode])
         outs.append(used)
-    scratch = refs
+    fetch_sems, *scratch = refs
+    rights, scratch = take(scratch, len(modes) - 1)
     products, reduces = [], []
     for number in range(len(modes)):
         used, scratch = take(scratch, 6)
-        products.append(Product(sides[2 * number], sides[2 * number + 1], used))
+        right = rights[number - 1] if number else sides[1]
+        products.append(Product(sides[2 * number], right, used))
+    loads = fetches(list(zip(sides[3::2], rights)), fetch_sems)
     for mode, count, product, out in zip(modes, spans, products, outs):
         parts = []
         if mode == "whole":
@@ -802,10 +818,14 @@
         reduces.append(parts)
     (out_sem,) = scratch
     products[0].load()
+    for load in loads:
+        load.start()
     greet()
     copies = []
     for number, product in enumerate(products):
         before = number and modes[number - 1] == "whole"
+        if number:
+            loads[number - 1].wait()
         product.send()
         if before:
             run(reduces[number - 1], "merge")
@@ -846,9 +866,13 @@
     out = pl.pallas_call(
         partial(weight_kernel, modes=modes, spans=tuple(spans)),
         out_shape=tuple(shapes),
-        in_specs=[ANY, VMEM] * len(pairs),
+        in_specs=[ANY, VMEM] + [ANY, ANY] * (len(pairs) - 1),
         out_specs=tuple(specs),
-        scratch_shapes=products + sums + [pltpu.SemaphoreType.DMA((1,))],
+        scratch_shapes=[pltpu.SemaphoreType.DMA((len(pairs),))]
+        + [pltpu.VMEM(right.shape, LOW) for _, right in pairs[1:]]
+        + products
+        + sums
+        + [pltpu.SemaphoreType.DMA((1,))],
         compiler_params=pltpu.CompilerParams(
             collective_id=number, has_side_effects=True, vmem_limit_bytes=63 * 2**20
         ),
@@ -877,22 +901,28 @@
 
 
 def last_kernel(*refs, spans):
-    slots, act, joint, x_ref, dx1_ref, table, weight, mid_sums, pre_sums, chooser = refs[:10]
+    slots, act, joint, x_hbm, dx1_hbm, weight_hbm, table, mid_sums, pre_sums, chooser = refs[:10]
     totals, refs = take(refs[10:], spans)
     qkv_out, fc1_out, small_w, x_grad_ref, *scratch = refs
     qkv_scratch, scratch = take(scratch, 6)
     qkv = Product(act, joint, qkv_scratch)
     qkv_sum, scratch = resident_reduces(qkv.sums, scratch)
     fc1_sum, scratch = far_reduces(totals, fc1_out.shape[0], scratch)
-    small_sends, small_receives, local, first_sums, joint_sums, small_s = scratch
+    small_sends, small_receives, local, first_sums, joint_sums, small_s, *scratch = scratch
+    x_ref, dx1_ref, weight, fetch_sems = scratch
+    loads = fetches(((x_hbm, x_ref), (dx1_hbm, dx1_ref), (weight_hbm, weight)), fetch_sems)
     small = Gather(small_w, small_sends, small_receives)
     tiles = x_ref.shape[0] // CHUNK
     qkv.load()
     greet()
     run(fc1_sum, "start_far")
+    for load in loads:
+        load.start()
     qkv.send()
     qkv.sum()
     run(qkv_sum, "start")
+    for load in loads:
+        load.wait()
 
     def back(at, carry):
         rows = pl.ds(pl.multiple_of(at * CHUNK, CHUNK), CHUNK)
@@ -965,7 +995,8 @@
             whole_shape(small_s),
             jax.ShapeDtypeStruct((tokens, D), WIDE),
         ),
-        in_specs=[pl.BlockSpec(memory_space=pltpu.SMEM), ANY] + [VMEM] * (8 + len(totals)),
+        in_specs=[pl.BlockSpec(memory_space=pltpu.SMEM), ANY, VMEM, ANY, ANY, ANY]
+        + [VMEM] * (4 + len(totals)),
         out_specs=(VMEM, VMEM, ANY, VMEM),
         scratch_shapes=Product.scratch(count, rows, tokens, columns)
         + resident_scratch((2, 2, count, rows, columns))
@@ -975,12 +1006,16 @@
             pltpu.VMEM((tokens // CHUNK, 8, D), WIDE),
             pltpu.VMEM((2, columns), WIDE),
             pltpu.VMEM(small_s.shape, LOW),
+            pltpu.VMEM(x_in.shape, LOW),
+            pltpu.VMEM(dx1.shape, WIDE),
+            pltpu.VMEM(weight.shape, LOW),
+            pltpu.SemaphoreType.DMA((3,)),
         ],
         compiler_params=pltpu.CompilerParams(
             collective_id=3, has_side_effects=True, vmem_limit_bytes=63 * 2**20
         ),
         name="last_scatter",
-    )(slots, act, joint, x_in, dx1, table, weight, mid_sums, pre_sums, chooser, *totals)
+    )(slots, act, joint, x_in, dx1, weight, table, mid_sums, pre_sums, chooser, *totals)
 
 
 def attend_back_kernel(*refs, counts):

time: 584 us -> 565 us (0.967)
  Pallas kernels: 525 us -> 508 us
    pallas_call x1, Pallas kernels: 127 us -> 116 us  [attend(): pl.pallas_call(attend_kernel, out_shape=(jax.ShapeDtypeStruct((wide, toke...]
where the time goes in v3:
time: 565 us; the launch traced here: 558 us
  Pallas kernels  508 us (90%)
  other arithmetic  23.9 us (4%)
  local copies, waits for them, and re-layouts  18.3 us (3%)
    pallas_call x1, Pallas kernels, attend(): pl.pallas_call(attend_kernel, out_shape=(jax.ShapeDtypeStruct((wide, toke...  116 us
    pallas_call x1, Pallas kernels, middle(): pl.pallas_call(middle_kernel, out_shape=tuple((jax.ShapeDtypeStruct(shape...  98.8 us
    pallas_call x1, Pallas kernels, first_gather(): pl.pallas_call(first_kernel, out_shape=tuple((whole_shape(shard) for shar...  83.6 us
    pallas_call x1, Pallas kernels, last_scatter(): pl.pallas_call(partial(last_kernel, spans=len(totals)), out_shape=(jax.Sh...  77.5 us
    pallas_call x1, Pallas kernels, attend_back(): pl.pallas_call(partial(attend_back_kernel, counts=(len(proj_totals), len(...  68.1 us
    pallas_call x1, Pallas kernels, weight_call(): pl.pallas_call(partial(weight_kernel, modes=modes, spans=tuple(spans)), o...  63.4 us
  transfers between devices with their start and end apart: 1, of which 0 were waited for; matrix products, arithmetic and copies ran while one was open for 3% of the time, Pallas kernels for 0%

profile of v3, /device:TPU:0, one launch (start us, length us, event | category | flops | bytes accessed | tf_op | source)
XLA Modules:
  0.0 558.2 jit_solution(237334013014115968)
XLA Ops:
  0.7 0.7 convert_element_type.49
  1.4 0.7 convert_element_type.54
  2.1 0.7 fusion.8
  2.8 0.1 reshape.151
  3.0 1.6 convert_element_type.51.refs_2_
  4.6 1.8 convert_element_type.50.refs_1_
  6.4 1.9 convert_element_type.52.refs_3_
  8.2 1.3 convert_element_type.53
  9.6 0.2 dynamic_update_slice.3
  9.8 1.0 fusion.2.refs_4_
  10.8 0.7 maximum_maximum_fusion.refs_0_
  11.4 83.6 %first_gather.1 = (bf16[2,4,2,2,8,768]{5,4,3,2,1,0:T(8,128)(2,1)}, bf16[2,4,2,2,72,1728]{5,4,3,2,1,0:T(8,128)(2,1)}, bf16[2,4,2,2,72,576]{5,4,3,2,1,0:T(8,128)(2...) custom-call(bf16[8,768]{1,0:T(8,128)(2,1)} %maximum_maximum_fusion.refs_0_, ...), custom_call_target="tpu_custom_call" | custom-call | tf_op jit(solution)/shard_map/first_gather/pallas_call | solution.py:293
  95.0 1.0 slice.36
  96.1 0.1 reshape.173.bias
  96.3 0.6 slice.40
  97.0 0.8 convert_element_type.58.refs_6_
  97.8 1.0 copy.63.refs_5_
  98.8 0.7 compare_convert_fusion.refs_9_
  99.4 1.6 constant_dynamic-slice_fusion.1
  101.0 0.6 fusion.14.refs_3_
  101.7 116.3 %attend.1 = (bf16[1152,1024]{1,0:T(8,128)(2,1)}, bf16[1024,1152]{1,0:T(8,128)(2,1)}, bf16[1152,1024]{1,0:T(8,128)(2,1)}, bf16[16,1024,128]{2,1,0:T(8,128)(2,1)},...) custom-call(s32[4]{0:T(128)} %copy-done.18, ...), custom_call_target="tpu_custom_call", output_to_operand_aliasing={{7}: (7, {}), {8}: (8, {})} | custom-call | tf_op jit(solution)/shard_map/attend/pallas_call | solution.py:443
  218.0 98.8 %middle.1 = (bf16[1024,1152]{1,0:T(8,128)(2,1)}, bf16[1152,1024]{1,0:T(8,128)(2,1)}, bf16[4608,1024]{1,0:T(8,128)(2,1)}, bf16[2,1024,2304]{2,1,0:T(8,128)(2,1)},...) custom-call(s32[4]{0:T(128)} %copy-done.18, ...), custom_call_target="tpu_custom_call" | custom-call | flops 48922361856 | bytes 71073792 | tf_op jit(solution)/shard_map/middle/pallas_call | solution.py:1303
  316.8 63.4 %weight_grads.1 = (bf16[4,40,576]{2,1,0:T(8,128)(2,1)}, bf16[4,32,576]{2,1,0:T(8,128)(2,1)}, bf16[4,144,576]{2,1,0:T(8,128)(2,1)}, bf16[4,144,576]{2,1,0:T(8,128...) custom-call(bf16[4,2,2,72,1024]{4,3,2,1,0:T(8,128)(2,1)} %bitcast.49, ...), custom_call_target="tpu_custom_call" | custom-call | tf_op jit(solution)/shard_map/weight_grads/pallas_call | solution.py:866
  380.2 68.1 %attend_back.1 = (bf16[2,1024,1728]{2,1,0:T(8,128)(2,1)}, f32[288,576]{1,0:T(8,128)}, f32[72,576]{1,0:T(8,128)}, bf16[4,40,2304]{2,1,0:T(8,128)(2,1)}, bf16[4,32,2304]{2,1,0:T(8,128)(2,1)}) custom-call(bf16[1024,1152]{1,0:T(8,128)(2,1)} %get-tuple-element.76.refs_0_, bf16[16,1024,128]{2,1,0:T(8,128)(2,1)} %get-tuple-element.77.refs_1_, ...), custom_call_target="tpu_custom_call" | custom-call | tf_op jit(solution)/shard_map/attend_back/pallas_call | solution.py:1135
  448.4 77.5 %last_scatter.1 = (f32[72,1728]{1,0:T(8,128)}, f32[72,2304]{1,0:T(8,128)}, bf16[2,4,2,2,16,3456]{5,4,3,2,1,0:T(8,128)(2,1)}, f32[1024,1152]{1,0:T(8,128)}) custom-call(s32[4]{0:T(128)} %copy-done.18, bf16[4,2,2,72,1024]{4,3,2,1,0:T(8,128)(2,1)} %bitcast.48, bf16[2,1024,1728]{2,1,0:T(8,128)(2,1)} %get-tuple-element.94.refs_2_, bf16[1024,1152]{1,0:T(8,128)(2,1)} %refs_3_.1, ...), custom_call_target="tpu_custom_call" | custom-call | tf_op jit(solution)/shard_map/last_scatter/pallas_call | solution.py:990
  525.9 1.9 copy_bitcast_fusion
  527.9 0.2 reshape.167
  528.1 0.4 fusion.3
  528.5 0.7 broadcast_in_dim.19
  529.2 4.0 all-to-all-start
  533.3 1.7 slice_bitcast_fusion
  535.0 1.7 slice.41
  536.7 0.2 reshape.171
  537.0 0.9 copy.68
  537.9 0.1 convert_reduce_fusion
  538.0 1.0 convert_reduce_fusion.1
  539.0 1.9 add_multiply_fusion.4
  540.9 0.6 add_multiply_fusion.5
  541.5 2.8 add_multiply_fusion.3
  544.3 1.5 add_multiply_fusion.2
  545.9 1.5 add_multiply_fusion.1
  547.4 0.7 copy-done.5
  548.1 0.3 copy-done.6
  548.5 2.2 add_multiply_fusion
  550.7 0.6 add_multiply_fusion.6
  551.3 0.9 bitcast_reduce_fusion
  552.3 0.6 fusion.10
  553.0 4.8 copy.76
  (65 shorter events, 0.5 us)
Async XLA Ops:
  3.0 93.9 %copy-start.19 = (s32[1024]{0:T(1024)S(1)}, s32[1024]{0:T(1024)}, u32[]{:S(2)}) copy-start(s32[1024]{0:T(1024)} %param.27) | copy-start | bytes 12292
  3.0 94.0 %copy-start.1 = (f32[288,576]{1,0:T(8,128)S(1)}, f32[288,576]{1,0:T(8,128)}, u32[]{:S(2)}) copy-start(f32[288,576]{1,0:T(8,128)} %param.38) | copy-start | bytes 1990660
  96.2 121.7 %copy-start.15 = (f32[1,9216]{1,0:T(1,128)}, f32[1,9216]{1,0:T(1,128)S(1)}, u32[]{:S(2)}) copy-start(f32[1,9216]{1,0:T(1,128)S(1)} %reshape.173.bias) | copy-start | bytes 110596
  97.0 4.7 copy-start.18
  528.1 10.9 %copy-start.10 = (f32[72,576]{1,0:T(8,128)S(1)}, f32[72,576]{1,0:T(8,128)}, u32[]{:S(2)}) copy-start(f32[72,576]{1,0:T(8,128)} %param.32) | copy-start | bytes 497668
  529.2 22.1 %all-to-all-start = ((f32[32,8,72]{2,1,0:T(8,128)}), f32[32,8,72]{2,1,0:T(8,128)}, u32[]{:S(2)}, u32[]{:S(2)}) async-start(f32[32,8,72]{2,1,0:T(8,128)} %bitcast.20), calls=%async_computation | async-start | bytes 262144 | tf_op jit(solution)/shard_map/all_to_all | solution.py:1480
  533.2 7.7 %copy-start.17 = (f32[288]{0:T(512)S(1)}, f32[288]{0:T(512)}, u32[]{:S(2)}) copy-start(f32[288]{0:T(512)} %param.41) | copy-start | bytes 3460
  533.2 7.7 %copy-start.21 = (f32[288]{0:T(512)S(1)}, f32[288]{0:T(512)}, u32[]{:S(2)}) copy-start(f32[288]{0:T(512)} %param.43) | copy-start | bytes 3460
  533.2 7.7 %copy-start.22 = (f32[288]{0:T(512)S(1)}, f32[288]{0:T(512)}, u32[]{:S(2)}) copy-start(f32[288]{0:T(512)} %param.42) | copy-start | bytes 3460
  533.3 8.3 %copy-start.4 = (f32[72,1728]{1,0:T(8,128)S(1)}, f32[72,1728]{1,0:T(8,128)}, u32[]{:S(2)}) copy-start(f32[72,1728]{1,0:T(8,128)} %param.29) | copy-start | bytes 1492996
  536.9 7.4 %copy-start.3 = (f32[72,2304]{1,0:T(8,128)S(1)}, f32[72,2304]{1,0:T(8,128)}, u32[]{:S(2)}) copy-start(f32[72,2304]{1,0:T(8,128)} %param.35) | copy-start | bytes 1990660
  537.9 6.5 %copy-start.11 = (f32[72,2304]{1,0:T(8,128)S(1)}, f32[72,2304]{1,0:T(8,128)}, u32[]{:S(2)}) copy-start(f32[72,2304]{1,0:T(8,128)} %param.37) | copy-start | bytes 1990660
  538.0 6.4 %copy-start.12 = (f32[72,2304]{1,0:T(8,128)S(1)}, f32[72,2304]{1,0:T(8,128)}, u32[]{:S(2)}) copy-start(f32[72,2304]{1,0:T(8,128)} %param.36) | copy-start | bytes 1990660
  538.0 6.3 %copy-start.13 = (f32[72,2304]{1,0:T(8,128)S(1)}, f32[72,2304]{1,0:T(8,128)}, u32[]{:S(2)}) copy-start(f32[72,2304]{1,0:T(8,128)} %get-tuple-element.104) | copy-start | bytes 1990660
  541.5 4.3 copy-start.2
  541.5 4.3 copy-start.7
  541.5 4.3 copy-start.8
  541.5 4.3 copy-start.9
  545.8 1.6 copy-start
  545.8 2.3 copy-start.5
  545.8 2.6 copy-start.6
  545.8 2.6 copy-start.14
  548.4 2.3 copy-start.20
  548.4 2.3 copy-start.23
  548.4 2.3 copy-start.24
  548.4 3.9 copy-start.16

commit v4 on v3

--- a/solution.py
+++ b/solution.py
@@ -255,9 +255,12 @@
 
 
 def first_kernel(*refs):
-    small_s, qkv_s, proj_s, fc1_s, ada = refs[:5]
+    small_s, *wide, ada = refs[:5]
     table = refs[9]
-    gather_sems, (local, *parts) = refs[10:18], refs[18:]
+    rounded, gather_sems, (local, *parts) = refs[10:13], refs[13:21], refs[21:]
+    qkv_s, proj_s, fc1_s = rounded
+    for source, target in zip(wide, rounded):
+        target[...] = source[...].astype(LOW)
     small, qkv, proj, fc1 = (
         Gather(w, s, r) for w, s, r in zip(refs[5:9], gather_sems[0::2], gather_sems[1::2])
     )
@@ -296,7 +299,8 @@
         + (jax.ShapeDtypeStruct((2, images, columns), WIDE),),
         in_specs=[VMEM] * 5,
         out_specs=(ANY,) * 5,
-        scratch_shapes=gather_scratch(4, 4)
+        scratch_shapes=[pltpu.VMEM(shard.shape, LOW) for shard in shards[1:]]
+        + gather_scratch(4, 4)
         + [
             pltpu.VMEM(small.shape, LOW),
             pltpu.VMEM((count, 2, 2, images, columns), WIDE),
@@ -511,6 +515,15 @@
             dict(far=target),
         )
 
+    def start_ahead(self):
+        self._both().start()
+        if self.first == "near":
+            self._first().start()
+
+    def start_rest(self):
+        if self.first == "mod":
+            self._first().start()
+
     def start(self):
         self._both().start()
         self._first().start()
@@ -728,6 +741,8 @@
         self.left, self.right = left, right
         self.rows_, self.sums, self.came, self.loads, self.sends, self.receives = scratch
         self.core = lax.axis_index("core")
+        near = lax.axis_index("near")
+        self.nears = (1 - near, near)
 
     @staticmethod
     def scratch(count, rows, tokens, columns):
@@ -742,7 +757,7 @@
         )
 
     def load(self):
-        for near in (0, 1):
+        for near in self.nears:
             self._load(near, 0).start()
 
     def _copy(self, mod, near):
@@ -768,7 +783,7 @@
                 store(mod, at, width, product.reshape(count, rows, width))
 
     def send(self):
-        for near in (0, 1):
+        for near in self.nears:
 
             def store(mod, at, width, product, near=near):
                 self.sums[mod, near, :, :, at : at + width] = product.astype(LOW)
@@ -778,8 +793,8 @@
             for mod in (0, 1):
                 self._copy(mod, near).start()
 
-    def sum(self):
-        for near in (0, 1):
+    def sum(self, reduces=()):
+        for near, names in zip(self.nears, ("start_ahead", "start_rest")):
             for mod in (0, 1):
                 self._copy(mod, near).wait_send()
                 self._copy(mod, near).wait_recv()
@@ -789,6 +804,7 @@
                 self.sums[mod, near, :, :, at : at + width] = (product + came.astype(WIDE)).astype(LOW)
 
             self._blocks(near, 1, store)
+            run(reduces, names)
 
 
 def total_shapes(count, rows, columns):
@@ -831,8 +847,7 @@
             run(reduces[number - 1], "merge")
         if number + 1 < len(products):
             products[number + 1].load()
-        product.sum()
-        run(reduces[number], "start") if reduces[number] else None
+        product.sum(reduces[number])
         if before:
             run(reduces[number - 1], "total")
         if modes[number] == "chip":
@@ -919,8 +934,7 @@
     for load in loads:
         load.start()
     qkv.send()
-    qkv.sum()
-    run(qkv_sum, "start")
+    qkv.sum(qkv_sum)
     for load in loads:
         load.wait()
 
@@ -1395,9 +1409,9 @@
     small_w, qkv_w, proj_w, fc1_w, table = first_gather(
         jnp.pad(ada_rows, ((0, LANES - ada_rows.shape[0]), (0, 0))),
         jnp.concatenate([half_silu, bias_block, blank], axis=1),
-        qkv_weight.astype(LOW),
-        proj_weight.astype(LOW),
-        fc1_weight.astype(LOW),
+        qkv_weight,
+        proj_weight,
+        fc1_weight,
     )
     small = small_w.reshape(2, row_devices * 8, -1)
     silu_all = jnp.concatenate([small[0, :, : width // 2], small[1, :, : width // 2]], axis=1)

time: 565 us -> 556 us (0.984)
  no operation moved by 1% of the time
where the time goes in v4:
time: 556 us; the launch traced here: 549 us
  Pallas kernels  504 us (91%)
  other arithmetic  18.7 us (3%)
  local copies, waits for them, and re-layouts  18.3 us (3%)
    pallas_call x1, Pallas kernels, attend(): pl.pallas_call(attend_kernel, out_shape=(jax.ShapeDtypeStruct((wide, toke...  116 us
    pallas_call x1, Pallas kernels, middle(): pl.pallas_call(middle_kernel, out_shape=tuple((jax.ShapeDtypeStruct(shape...  98.8 us
    pallas_call x1, Pallas kernels, first_gather(): pl.pallas_call(first_kernel, out_shape=tuple((whole_shape(shard) for shar...  83.8 us
    pallas_call x1, Pallas kernels, last_scatter(): pl.pallas_call(partial(last_kernel, spans=len(totals)), out_shape=(jax.Sh...  74.6 us
    pallas_call x1, Pallas kernels, attend_back(): pl.pallas_call(partial(attend_back_kernel, counts=(len(proj_totals), len(...  68.7 us
    pallas_call x1, Pallas kernels, weight_call(): pl.pallas_call(partial(weight_kernel, modes=modes, spans=tuple(spans)), o...  61.3 us
  transfers between devices with their start and end apart: 1, of which 0 were waited for; matrix products, arithmetic and copies ran while one was open for 3% of the time, Pallas kernels for 0%

profile of v4, /device:TPU:0, one launch (start us, length us, event | category | flops | bytes accessed | tf_op | source)
XLA Modules:
  0.0 548.6 jit_solution(17889847199142364538)
XLA Ops:
  0.7 0.8 convert_element_type.40
  1.5 0.7 convert_element_type.42
  2.1 0.7 fusion.8
  2.9 0.1 reshape.151
  3.0 1.3 convert_element_type.41
  4.3 0.1 pad.19.clone
  4.4 0.2 dynamic_update_slice.3
  4.6 1.0 fusion.2.refs_4_
  5.6 0.7 maximum_maximum_fusion.refs_0_
  6.2 83.8 %first_gather.1 = (bf16[2,4,2,2,8,768]{5,4,3,2,1,0:T(8,128)(2,1)}, bf16[2,4,2,2,72,1728]{5,4,3,2,1,0:T(8,128)(2,1)}, bf16[2,4,2,2,72,576]{5,4,3,2,1,0:T(8,128)(2...) custom-call(bf16[8,768]{1,0:T(8,128)(2,1)} %maximum_maximum_fusion.refs_0_, f32[72,1728]{1,0:T(8,128)} %refs_1_.2, ...), custom_call_target="tpu_custom_call" | custom-call | tf_op jit(solution)/shard_map/first_gather/pallas_call | solution.py:296
  90.0 1.0 slice.36
  91.1 0.1 reshape.173.bias
  91.3 0.6 slice.40
  91.9 0.1 slice.27.refs_0_.slots
  92.0 0.8 convert_element_type.46.refs_6_
  92.8 1.0 copy.63.refs_5_
  93.8 0.7 compare_convert_fusion.refs_9_
  94.5 1.6 constant_dynamic-slice_fusion.1
  96.1 0.6 fusion.14.refs_3_
  96.7 116.3 %attend.1 = (bf16[1152,1024]{1,0:T(8,128)(2,1)}, bf16[1024,1152]{1,0:T(8,128)(2,1)}, bf16[1152,1024]{1,0:T(8,128)(2,1)}, bf16[16,1024,128]{2,1,0:T(8,128)(2,1)},...) custom-call(s32[4]{0:T(128)} %copy-done.18, ...), custom_call_target="tpu_custom_call", output_to_operand_aliasing={{7}: (7, {}), {8}: (8, {})} | custom-call | tf_op jit(solution)/shard_map/attend/pallas_call | solution.py:447
  213.0 98.8 %middle.1 = (bf16[1024,1152]{1,0:T(8,128)(2,1)}, bf16[1152,1024]{1,0:T(8,128)(2,1)}, bf16[4608,1024]{1,0:T(8,128)(2,1)}, bf16[2,1024,2304]{2,1,0:T(8,128)(2,1)},...) custom-call(s32[4]{0:T(128)} %copy-done.18, ...), custom_call_target="tpu_custom_call" | custom-call | flops 48922361856 | bytes 71073792 | tf_op jit(solution)/shard_map/middle/pallas_call | solution.py:1317
  311.8 61.3 %weight_grads.1 = (bf16[4,40,576]{2,1,0:T(8,128)(2,1)}, bf16[4,32,576]{2,1,0:T(8,128)(2,1)}, bf16[4,144,576]{2,1,0:T(8,128)(2,1)}, bf16[4,144,576]{2,1,0:T(8,128...) custom-call(bf16[4,2,2,72,1024]{4,3,2,1,0:T(8,128)(2,1)} %bitcast.49, ...), custom_call_target="tpu_custom_call" | custom-call | tf_op jit(solution)/shard_map/weight_grads/pallas_call | solution.py:881
  373.2 68.7 %attend_back.1 = (bf16[2,1024,1728]{2,1,0:T(8,128)(2,1)}, f32[288,576]{1,0:T(8,128)}, f32[72,576]{1,0:T(8,128)}, bf16[4,40,2304]{2,1,0:T(8,128)(2,1)}, bf16[4,32,2304]{2,1,0:T(8,128)(2,1)}) custom-call(bf16[1024,1152]{1,0:T(8,128)(2,1)} %get-tuple-element.76.refs_0_, bf16[16,1024,128]{2,1,0:T(8,128)(2,1)} %get-tuple-element.77.refs_1_, ...), custom_call_target="tpu_custom_call" | custom-call | tf_op jit(solution)/shard_map/attend_back/pallas_call | solution.py:1149
  441.9 74.6 %last_scatter.1 = (f32[72,1728]{1,0:T(8,128)}, f32[72,2304]{1,0:T(8,128)}, bf16[2,4,2,2,16,3456]{5,4,3,2,1,0:T(8,128)(2,1)}, f32[1024,1152]{1,0:T(8,128)}) custom-call(s32[4]{0:T(128)} %copy-done.18, bf16[4,2,2,72,1024]{4,3,2,1,0:T(8,128)(2,1)} %bitcast.48, bf16[2,1024,1728]{2,1,0:T(8,128)(2,1)} %get-tuple-element.94.refs_2_, bf16[1024,1152]{1,0:T(8,128)(2,1)} %refs_3_.3, ...), custom_call_target="tpu_custom_call" | custom-call | tf_op jit(solution)/shard_map/last_scatter/pallas_call | solution.py:1004
  516.5 1.9 copy_bitcast_fusion
  518.5 0.2 reshape.167
  518.7 0.4 fusion.3
  519.1 0.7 broadcast_in_dim.19
  519.8 3.8 all-to-all-start
  523.7 1.7 slice_bitcast_fusion
  525.4 1.7 slice.41
  527.1 0.2 reshape.171
  527.4 0.9 copy.68
  528.3 0.1 convert_reduce_fusion
  528.4 1.0 convert_reduce_fusion.1
  529.4 1.9 add_multiply_fusion.4
  531.3 0.6 add_multiply_fusion.5
  531.9 2.8 add_multiply_fusion.3
  534.7 1.5 add_multiply_fusion.2
  536.3 1.5 add_multiply_fusion.1
  537.8 0.7 copy-done.5
  538.5 0.3 copy-done.6
  538.9 2.2 add_multiply_fusion
  541.1 0.6 add_multiply_fusion.6
  541.7 0.9 bitcast_reduce_fusion
  542.6 0.1 reshape.169
  542.7 0.6 fusion.10
  543.4 4.8 copy.76
  (62 shorter events, 0.3 us)
Async XLA Ops:
  0.7 91.2 %copy-start.19 = (s32[1024]{0:T(1024)S(1)}, s32[1024]{0:T(1024)}, u32[]{:S(2)}) copy-start(s32[1024]{0:T(1024)} %param.27) | copy-start | bytes 12292
  0.7 91.3 %copy-start.1 = (f32[288,576]{1,0:T(8,128)S(1)}, f32[288,576]{1,0:T(8,128)}, u32[]{:S(2)}) copy-start(f32[288,576]{1,0:T(8,128)} %param.38) | copy-start | bytes 1990660
  91.3 121.7 %copy-start.15 = (f32[1,9216]{1,0:T(1,128)}, f32[1,9216]{1,0:T(1,128)S(1)}, u32[]{:S(2)}) copy-start(f32[1,9216]{1,0:T(1,128)S(1)} %reshape.173.bias) | copy-start | bytes 110596
  92.0 4.7 copy-start.18
  518.7 10.7 %copy-start.10 = (f32[72,576]{1,0:T(8,128)S(1)}, f32[72,576]{1,0:T(8,128)}, u32[]{:S(2)}) copy-start(f32[72,576]{1,0:T(8,128)} %refs_2_.1) | copy-start | bytes 497668
  519.8 21.9 %all-to-all-start = ((f32[32,8,72]{2,1,0:T(8,128)}), f32[32,8,72]{2,1,0:T(8,128)}, u32[]{:S(2)}, u32[]{:S(2)}) async-start(f32[32,8,72]{2,1,0:T(8,128)} %bitcast.20), calls=%async_computation | async-start | bytes 262144 | tf_op jit(solution)/shard_map/all_to_all | solution.py:1494
  523.6 7.7 %copy-start.17 = (f32[288]{0:T(512)S(1)}, f32[288]{0:T(512)}, u32[]{:S(2)}) copy-start(f32[288]{0:T(512)} %param.41) | copy-start | bytes 3460
  523.6 7.7 %copy-start.21 = (f32[288]{0:T(512)S(1)}, f32[288]{0:T(512)}, u32[]{:S(2)}) copy-start(f32[288]{0:T(512)} %param.43) | copy-start | bytes 3460
  523.6 7.7 %copy-start.22 = (f32[288]{0:T(512)S(1)}, f32[288]{0:T(512)}, u32[]{:S(2)}) copy-start(f32[288]{0:T(512)} %param.42) | copy-start | bytes 3460
  523.7 8.3 %copy-start.4 = (f32[72,1728]{1,0:T(8,128)S(1)}, f32[72,1728]{1,0:T(8,128)}, u32[]{:S(2)}) copy-start(f32[72,1728]{1,0:T(8,128)} %refs_1_.2) | copy-start | bytes 1492996
  527.3 7.4 %copy-start.3 = (f32[72,2304]{1,0:T(8,128)S(1)}, f32[72,2304]{1,0:T(8,128)}, u32[]{:S(2)}) copy-start(f32[72,2304]{1,0:T(8,128)} %refs_3_.2) | copy-start | bytes 1990660
  528.3 6.5 %copy-start.11 = (f32[72,2304]{1,0:T(8,128)S(1)}, f32[72,2304]{1,0:T(8,128)}, u32[]{:S(2)}) copy-start(f32[72,2304]{1,0:T(8,128)} %param.37) | copy-start | bytes 1990660
  528.4 6.4 %copy-start.12 = (f32[72,2304]{1,0:T(8,128)S(1)}, f32[72,2304]{1,0:T(8,128)}, u32[]{:S(2)}) copy-start(f32[72,2304]{1,0:T(8,128)} %param.36) | copy-start | bytes 1990660
  528.4 6.3 %copy-start.13 = (f32[72,2304]{1,0:T(8,128)S(1)}, f32[72,2304]{1,0:T(8,128)}, u32[]{:S(2)}) copy-start(f32[72,2304]{1,0:T(8,128)} %get-tuple-element.104) | copy-start | bytes 1990660
  531.9 4.3 copy-start.2
  531.9 4.3 copy-start.7
  531.9 4.3 copy-start.8
  531.9 4.3 copy-start.9
  536.2 1.6 copy-start
  536.2 2.3 copy-start.5
  536.2 2.6 copy-start.6
  536.2 2.6 copy-start.14
  538.8 2.3 copy-start.20
  538.8 2.3 copy-start.23
  538.8 2.3 copy-start.24
  538.8 3.9 copy-start.16

commit v5 on v4

--- a/solution.py
+++ b/solution.py
@@ -1177,7 +1177,7 @@
 
 
 def row_of(table, slot, group):
-    return table[pl.ds(slot, 1), group * D : (group + 1) * D]
+    return table[group // 3, pl.ds(slot, 1), group % 3 * D : (group % 3 + 1) * D]
 
 
 def column_sums(values):
@@ -1417,14 +1417,12 @@
     silu_all = jnp.concatenate([small[0, :, : width // 2], small[1, :, : width // 2]], axis=1)
     bias_all = small[:, :, width // 2 : width // 2 + LANES].reshape(2, row_devices, -1)
     bias_full = jnp.swapaxes(bias_all[:, :, :own_bias], 0, 1).reshape(1, -1).astype(WIDE)
-    table = lax.dynamic_slice_in_dim(table, lax.axis_index("mod") * images, images, 1)
-    table = jnp.swapaxes(table, 0, 1).reshape(images, -1)
-
     def joined(whole):
         return whole.reshape(2, -1, whole.shape[-1])
 
     qkv_low = joined(qkv_w)
     slots = segments[::CHUNK]
+    table_rows = slots + lax.axis_index("mod") * images
     joint_bias = jnp.concatenate(
         [bias_full[:, 0:width], jnp.zeros((1, width), WIDE), bias_full[:, width : 2 * width]], axis=1
     )
@@ -1432,7 +1430,7 @@
         return turned.reshape(row_devices // 4, 2, 2, -1, tokens)
 
     act_turned, mixture, mixture_turned, heads, (proj_w, fc1_w, fc2_w) = attend(
-        slots,
+        table_rows,
         x_in,
         table,
         joint_bias,
@@ -1445,7 +1443,7 @@
     (
         block_out, mlp_turned, hidden_turned, pre_halves, branch_halves, attn_halves, mixture_grad, middle_grad, sums, pre_sums,
     ) = middle(
-        slots, x_in, out_grad, mixture, table, bias_full, joined(proj_w), joined(fc1_w), joined(fc2_w)
+        table_rows, x_in, out_grad, mixture, table, bias_full, joined(proj_w), joined(fc1_w), joined(fc2_w)
     )
     proj_totals, fc2_joints, fc2_bases, fc1_sums = weight_grads(
         blocked(hidden_turned),
@@ -1460,7 +1458,7 @@
     )
     chooser = (slots[None, :] == (jnp.arange(2 * images, dtype=jnp.int32) % images)[:, None]).astype(WIDE)
     qkv_shard, fc1_shard, small_grads, x_grad = last_scatter(
-        slots,
+        table_rows,
         blocked(act_turned),
         joint_halves,
         x_in,

time: 556 us -> 554 us (level)
  no operation moved by 1% of the time
where the time goes in v5:
time: 554 us; the launch traced here: 547 us
  Pallas kernels  504 us (91%)
  other arithmetic  19.3 us (3%)
  local copies, waits for them, and re-layouts  15.7 us (3%)
    pallas_call x1, Pallas kernels, attend(): pl.pallas_call(attend_kernel, out_shape=(jax.ShapeDtypeStruct((wide, toke...  116 us
    pallas_call x1, Pallas kernels, middle(): pl.pallas_call(middle_kernel, out_shape=tuple((jax.ShapeDtypeStruct(shape...  98.8 us
    pallas_call x1, Pallas kernels, first_gather(): pl.pallas_call(first_kernel, out_shape=tuple((whole_shape(shard) for shar...  83.8 us
    pallas_call x1, Pallas kernels, last_scatter(): pl.pallas_call(partial(last_kernel, spans=len(totals)), out_shape=(jax.Sh...  74.7 us
    pallas_call x1, Pallas kernels, attend_back(): pl.pallas_call(partial(attend_back_kernel, counts=(len(proj_totals), len(...  68.7 us
    pallas_call x1, Pallas kernels, weight_call(): pl.pallas_call(partial(weight_kernel, modes=modes, spans=tuple(spans)), o...  61.4 us
  transfers between devices with their start and end apart: 1, of which 0 were waited for; matrix products, arithmetic and copies ran while one was open for 3% of the time, Pallas kernels for 0%

profile of v5, /device:TPU:0, one launch (start us, length us, event | category | flops | bytes accessed | tf_op | source)
XLA Modules:
  0.0 546.6 jit_solution(12361275668046695966)
XLA Ops:
  0.7 0.8 convert_element_type.40
  1.5 0.7 convert_element_type.42
  2.1 0.7 fusion.8
  2.9 0.1 reshape.148
  3.0 1.3 convert_element_type.41
  4.3 0.1 pad.19.clone
  4.4 0.2 dynamic_update_slice.3
  4.6 1.0 fusion.2.refs_4_
  5.6 0.7 maximum_maximum_fusion.refs_0_
  6.2 83.8 %first_gather.1 = (bf16[2,4,2,2,8,768]{5,4,3,2,1,0:T(8,128)(2,1)}, bf16[2,4,2,2,72,1728]{5,4,3,2,1,0:T(8,128)(2,1)}, bf16[2,4,2,2,72,576]{5,4,3,2,1,0:T(8,128)(2...) custom-call(bf16[8,768]{1,0:T(8,128)(2,1)} %maximum_maximum_fusion.refs_0_, f32[72,1728]{1,0:T(8,128)} %refs_1_.2, ...), custom_call_target="tpu_custom_call" | custom-call | tf_op jit(solution)/shard_map/first_gather/pallas_call | solution.py:296
  90.0 1.0 slice.36
  91.1 0.1 reshape.169.bias
  91.3 0.6 slice.40
  91.9 0.1 slice.27
  92.0 0.5 broadcast_add_fusion.refs_0_.slots
  92.5 0.7 compare_convert_fusion.refs_9_
  93.2 0.8 convert_element_type.46.refs_6_
  93.9 1.0 copy.63.refs_5_
  95.0 0.6 fusion.14.refs_3_
  95.6 116.3 %attend.1 = (bf16[1152,1024]{1,0:T(8,128)(2,1)}, bf16[1024,1152]{1,0:T(8,128)(2,1)}, bf16[1152,1024]{1,0:T(8,128)(2,1)}, bf16[16,1024,128]{2,1,0:T(8,128)(2,1)},...) custom-call(s32[4]{0:T(128)} %broadcast_add_fusion.refs_0_.slots, ...), custom_call_target="tpu_custom_call", output_to_operand_aliasing={{7}: (7, {}), {8}: (8, {})} | custom-call | tf_op jit(solution)/shard_map/attend/pallas_call | solution.py:447
  211.9 98.8 %middle.1 = (bf16[1024,1152]{1,0:T(8,128)(2,1)}, bf16[1152,1024]{1,0:T(8,128)(2,1)}, bf16[4608,1024]{1,0:T(8,128)(2,1)}, bf16[2,1024,2304]{2,1,0:T(8,128)(2,1)},...) custom-call(s32[4]{0:T(128)} %broadcast_add_fusion.refs_0_.slots, ...), custom_call_target="tpu_custom_call" | custom-call | flops 48922361856 | bytes 71073792 | tf_op jit(solution)/shard_map/middle/pallas_call | solution.py:1317
  310.7 61.4 %weight_grads.1 = (bf16[4,40,576]{2,1,0:T(8,128)(2,1)}, bf16[4,32,576]{2,1,0:T(8,128)(2,1)}, bf16[4,144,576]{2,1,0:T(8,128)(2,1)}, bf16[4,144,576]{2,1,0:T(8,128...) custom-call(bf16[4,2,2,72,1024]{4,3,2,1,0:T(8,128)(2,1)} %bitcast.46, ...), custom_call_target="tpu_custom_call" | custom-call | tf_op jit(solution)/shard_map/weight_grads/pallas_call | solution.py:881
  372.1 68.7 %attend_back.1 = (bf16[2,1024,1728]{2,1,0:T(8,128)(2,1)}, f32[288,576]{1,0:T(8,128)}, f32[72,576]{1,0:T(8,128)}, bf16[4,40,2304]{2,1,0:T(8,128)(2,1)}, bf16[4,32,2304]{2,1,0:T(8,128)(2,1)}) custom-call(bf16[1024,1152]{1,0:T(8,128)(2,1)} %get-tuple-element.76.refs_0_, bf16[16,1024,128]{2,1,0:T(8,128)(2,1)} %get-tuple-element.77.refs_1_, ...), custom_call_target="tpu_custom_call" | custom-call | tf_op jit(solution)/shard_map/attend_back/pallas_call | solution.py:1149
  440.8 74.7 %last_scatter.1 = (f32[72,1728]{1,0:T(8,128)}, f32[72,2304]{1,0:T(8,128)}, bf16[2,4,2,2,16,3456]{5,4,3,2,1,0:T(8,128)(2,1)}, f32[1024,1152]{1,0:T(8,128)}) custom-call(s32[4]{0:T(128)} %broadcast_add_fusion.refs_0_.slots, bf16[4,2,2,72,1024]{4,3,2,1,0:T(8,128)(2,1)} %bitcast.45, bf16[2,1024,1728]{2,1,0:T(8,128)(2,1)} %get-tuple-element.94.refs_2_, ...), custom_call_target="tpu_custom_call" | custom-call | tf_op jit(solution)/shard_map/last_scatter/pallas_call | solution.py:1004
  515.5 2.0 copy_bitcast_fusion
  517.5 0.2 reshape.163
  517.7 0.4 fusion.3
  518.1 0.7 broadcast_in_dim.19
  518.8 3.8 all-to-all-start
  522.7 0.7 slice_bitcast_fusion
  523.4 1.7 slice.41
  525.1 0.2 reshape.167
  525.3 0.9 copy.68
  526.2 0.1 convert_reduce_fusion
  526.4 1.0 convert_reduce_fusion.1
  527.4 1.9 add_multiply_fusion.4
  529.3 0.6 add_multiply_fusion.5
  530.0 2.8 add_multiply_fusion.3
  532.7 1.5 add_multiply_fusion.2
  534.3 1.6 add_multiply_fusion.1
  535.8 0.7 copy-done.5
  536.5 0.3 copy-done.6
  536.9 2.2 add_multiply_fusion
  539.1 0.6 add_multiply_fusion.6
  539.7 0.9 bitcast_reduce_fusion
  540.6 0.1 reshape.165
  540.7 0.6 fusion.10
  541.4 4.8 copy.76
  (62 shorter events, 0.3 us)
Async XLA Ops:
  0.7 91.2 %copy-start.19 = (s32[1024]{0:T(1024)S(1)}, s32[1024]{0:T(1024)}, u32[]{:S(2)}) copy-start(s32[1024]{0:T(1024)} %param.27) | copy-start | bytes 12292
  0.7 92.5 %copy-start.1 = (f32[288,576]{1,0:T(8,128)S(1)}, f32[288,576]{1,0:T(8,128)}, u32[]{:S(2)}) copy-start(f32[288,576]{1,0:T(8,128)} %param.38) | copy-start | bytes 1990660
  91.3 120.7 %copy-start.16 = (f32[1,9216]{1,0:T(1,128)}, f32[1,9216]{1,0:T(1,128)S(1)}, u32[]{:S(2)}) copy-start(f32[1,9216]{1,0:T(1,128)S(1)} %reshape.169.bias) | copy-start | bytes 110596
  515.5 7.1 %copy-start.15 = (bf16[2,4,2,2,8,768]{5,4,3,2,1,0:T(8,128)(2,1)S(1)}, bf16[2,4,2,2,8,768]{5,4,3,2,1,0:T(8,128)(2,1)}, u32[]{:S(2)}) copy-start(bf16[2,4,2,2,8,768]{5,4,3,2,1,0:T(8,128)(2,1)} %get-tuple-element.66) | copy-start | bytes 1179652
  517.7 9.7 %copy-start.10 = (f32[72,576]{1,0:T(8,128)S(1)}, f32[72,576]{1,0:T(8,128)}, u32[]{:S(2)}) copy-start(f32[72,576]{1,0:T(8,128)} %refs_2_.1) | copy-start | bytes 497668
  518.8 20.9 %all-to-all-start = ((f32[32,8,72]{2,1,0:T(8,128)}), f32[32,8,72]{2,1,0:T(8,128)}, u32[]{:S(2)}, u32[]{:S(2)}) async-start(f32[32,8,72]{2,1,0:T(8,128)} %bitcast.17), calls=%async_computation | async-start | bytes 262144 | tf_op jit(solution)/shard_map/all_to_all | solution.py:1492
  522.6 6.7 %copy-start.18 = (f32[288]{0:T(512)S(1)}, f32[288]{0:T(512)}, u32[]{:S(2)}) copy-start(f32[288]{0:T(512)} %param.41) | copy-start | bytes 3460
  522.7 6.7 %copy-start.21 = (f32[288]{0:T(512)S(1)}, f32[288]{0:T(512)}, u32[]{:S(2)}) copy-start(f32[288]{0:T(512)} %param.43) | copy-start | bytes 3460
  522.7 6.7 %copy-start.22 = (f32[288]{0:T(512)S(1)}, f32[288]{0:T(512)}, u32[]{:S(2)}) copy-start(f32[288]{0:T(512)} %param.42) | copy-start | bytes 3460
  522.7 7.3 %copy-start.4 = (f32[72,1728]{1,0:T(8,128)S(1)}, f32[72,1728]{1,0:T(8,128)}, u32[]{:S(2)}) copy-start(f32[72,1728]{1,0:T(8,128)} %refs_1_.2) | copy-start | bytes 1492996
  525.3 7.4 %copy-start.3 = (f32[72,2304]{1,0:T(8,128)S(1)}, f32[72,2304]{1,0:T(8,128)}, u32[]{:S(2)}) copy-start(f32[72,2304]{1,0:T(8,128)} %refs_3_.2) | copy-start | bytes 1990660
  526.3 6.4 %copy-start.11 = (f32[72,2304]{1,0:T(8,128)S(1)}, f32[72,2304]{1,0:T(8,128)}, u32[]{:S(2)}) copy-start(f32[72,2304]{1,0:T(8,128)} %param.37) | copy-start | bytes 1990660
  526.4 6.4 %copy-start.12 = (f32[72,2304]{1,0:T(8,128)S(1)}, f32[72,2304]{1,0:T(8,128)}, u32[]{:S(2)}) copy-start(f32[72,2304]{1,0:T(8,128)} %param.36) | copy-start | bytes 1990660
  526.4 6.4 %copy-start.13 = (f32[72,2304]{1,0:T(8,128)S(1)}, f32[72,2304]{1,0:T(8,128)}, u32[]{:S(2)}) copy-start(f32[72,2304]{1,0:T(8,128)} %get-tuple-element.104) | copy-start | bytes 1990660
  529.9 4.3 copy-start.2
  529.9 4.3 copy-start.7
  529.9 4.3 copy-start.8
  529.9 4.3 copy-start.9
  534.2 1.6 copy-start
  534.2 2.3 copy-start.5
  534.2 2.6 copy-start.6
  534.2 2.6 copy-start.14
  536.8 2.3 copy-start.20
  536.8 2.3 copy-start.23
  536.8 2.3 copy-start.24
  536.8 3.9 copy-start.17
